TPU v7x, 32 devices: a whole 2x2x4 slice. The times are simulated.
32 devices in a mesh: ctx: 8 (over y, x, core), fsdp: 4 (over z).
Axes of the slice: x: 2, y: 2, z: 4, core: 2. Of those that a mesh axis runs over, the one named last changes fastest.
Arguments:
- layer_in: float32 [4, 1024, 1024], P('fsdp', 'ctx'), may hold values from -6 to 6
- attention_norm_gain: bfloat16 [1024], P('fsdp'), may hold values from 0.5 to 1.5
- attention_norm_bias: bfloat16 [1024], P('fsdp'), may hold values from -1 to 1
- feedforward_norm_gain: bfloat16 [1024], P('fsdp'), may hold values from 0.5 to 1.5
- feedforward_norm_bias: bfloat16 [1024], P('fsdp'), may hold values from -1 to 1
- qkv_weight: bfloat16 [1024, 3072], P('fsdp'), may hold values from -0.1875 to 0.1875
- qkv_bias: bfloat16 [3072], P('fsdp'), may hold values from -2.5 to 2.5
- out_weight: bfloat16 [1024, 1024], P('fsdp'), may hold values from -4 to 4
- out_bias: bfloat16 [1024], P('fsdp'), may hold values from -1 to 1
- fc1_weight: bfloat16 [1024, 4096], P('fsdp'), may hold values from -0.1875 to 0.1875
- fc1_bias: bfloat16 [4096], P('fsdp'), may hold values from -2.5 to 2.5
- fc2_weight: bfloat16 [4096, 1024], P('fsdp'), may hold values from -0.09375 to 0.09375
- fc2_bias: bfloat16 [1024], P('fsdp'), may hold values from -1 to 1
- cotangent: float32 [4, 1024, 1024], P('fsdp', 'ctx'), may hold values from -6 to 6
Outputs:
- layer_out: float32 [4, 1024, 1024], P('fsdp', 'ctx')
- in_grad: float32 [4, 1024, 1024], P('fsdp', 'ctx')
- grad_ln1_gain: float32 [1024], P('fsdp')
- grad_ln1_bias: float32 [1024], P('fsdp')
- grad_ln2_gain: float32 [1024], P('fsdp')
- grad_ln2_bias: float32 [1024], P('fsdp')
- grad_qkv_weight: float32 [1024, 3072], P('fsdp')
- grad_qkv_bias: float32 [3072], P('fsdp')
- grad_out_weight: float32 [1024, 1024], P('fsdp')
- grad_out_bias: float32 [1024], P('fsdp')
- grad_fc1_weight: float32 [1024, 4096], P('fsdp')
- grad_fc1_bias: float32 [4096], P('fsdp')
- grad_fc2_weight: float32 [4096, 1024], P('fsdp')
- grad_fc2_bias: float32 [1024], P('fsdp')
All inputs are finite; a program needn't handle non-finite values.
Results may differ from a plain program's by a relative error of at most 0.02.
Values may be sent and summed in bfloat16 or wider, within the bound.
A program may use at most 192 MiB of HBM per device.

v0:
```python
import math

import jax
import jax.numpy as jnp
from jax import lax
from jax.sharding import PartitionSpec as P

H = 16
HD = 64
ROT = 16


norm_eps = 1e-05
masked_score = -1e30
root_half = 1.0 / math.sqrt(2.0)
root_two_pi = 1.0 / math.sqrt(2.0 * math.pi)


def from_behind(array, axis, by):
    devices = lax.axis_size(axis)
    return lax.ppermute(array, axis, [(i, (i + by) % devices) for i in range(devices)])


def layernorm_forward(values_in, gain_vec, offset):
    centered = values_in - jnp.mean(values_in, axis=1, keepdims=True)
    inv_scale = lax.rsqrt(jnp.mean(centered * centered, axis=1, keepdims=True) + norm_eps)
    normed = centered * inv_scale
    return (normed * gain_vec.astype(jnp.float32) + offset.astype(jnp.float32), normed, inv_scale)


def layernorm_backward(grad_out, normed, inv_scale, gain_vec):
    scaled = grad_out * gain_vec.astype(jnp.float32)
    return inv_scale * (
        scaled
        - jnp.mean(scaled, axis=1, keepdims=True)
        - normed * jnp.mean(scaled * normed, axis=1, keepdims=True)
    )


def gelu_value(inputs):
    return 0.5 * inputs * (1.0 + lax.erf(inputs * root_half))


def gelu_slope(inputs):
    return (
        0.5 * (1.0 + lax.erf(inputs * root_half))
        + inputs * jnp.exp(-0.5 * inputs * inputs) * root_two_pi
    )


def angle_tables(positions):
    halfway = ROT // 2
    freqs = jnp.power(10000.0, -2.0 * jnp.arange(halfway, dtype=jnp.float32) / ROT)
    angles = positions.astype(jnp.float32)[:, None] * freqs[None, :]
    return (jnp.cos(angles), jnp.sin(angles))


def split_heads(matrix):
    return matrix.reshape(matrix.shape[0], H, HD)


def rotate_heads(block, cos_table, sin_table):
    halfway = ROT // 2
    leading = block[..., :halfway]
    trailing = block[..., halfway:ROT]
    cos_part = cos_table[:, None, :]
    sin_part = sin_table[:, None, :]
    return jnp.concatenate(
        [
            leading * cos_part - trailing * sin_part,
            trailing * cos_part + leading * sin_part,
            block[..., ROT:],
        ],
        axis=-1,
    )


def unrotate_heads(block, cos_table, sin_table):
    halfway = ROT // 2
    leading = block[..., :halfway]
    trailing = block[..., halfway:ROT]
    cos_part = cos_table[:, None, :]
    sin_part = sin_table[:, None, :]
    return jnp.concatenate(
        [
            leading * cos_part + trailing * sin_part,
            trailing * cos_part - leading * sin_part,
            block[..., ROT:],
        ],
        axis=-1,
    )


def block_forward(queries, key_block, value_block, query_pos, key_pos):
    scores = jnp.einsum(
        "qhd,khd->hqk",
        split_heads(queries),
        split_heads(key_block),
        preferred_element_type=jnp.float32,
    ) * HD ** (-0.5)
    visible = (query_pos[:, None] >= key_pos[None, :])[None]
    scores = jnp.where(visible, scores, masked_score)
    highest = jnp.max(scores, axis=2)
    weights = jnp.where(visible, jnp.exp(scores - highest[..., None]), 0.0)
    mixture = jnp.einsum(
        "hqk,khd->hqd",
        weights.astype(jnp.bfloat16),
        split_heads(value_block),
        preferred_element_type=jnp.float32,
    )
    return (mixture, highest, jnp.sum(weights, axis=2))


def merge_state(state, update):
    summed, highest, totals = state
    part_sum, part_high, part_total = update
    newest = jnp.maximum(highest, part_high)
    old_factor = jnp.exp(highest - newest)
    new_factor = jnp.exp(part_high - newest)
    return (
        summed * old_factor[..., None] + part_sum * new_factor[..., None],
        newest,
        totals * old_factor + part_total * new_factor,
    )


def block_backward(
    queries, key_block, value_block, grad_mix, log_total, delta_sum, query_pos, key_pos
):
    query_heads = split_heads(queries)
    key_heads = split_heads(key_block)
    value_heads = split_heads(value_block)
    grad_heads = split_heads(grad_mix)
    scores = jnp.einsum(
        "qhd,khd->hqk", query_heads, key_heads, preferred_element_type=jnp.float32
    ) * HD ** (-0.5)
    visible = (query_pos[:, None] >= key_pos[None, :])[None]
    probs = jnp.where(
        visible, jnp.exp(jnp.where(visible, scores, masked_score) - log_total[..., None]), 0.0
    )
    value_grad = jnp.einsum(
        "hqk,qhd->khd", probs.astype(jnp.bfloat16), grad_heads, preferred_element_type=jnp.float32
    )
    prob_grad = jnp.einsum(
        "qhd,khd->hqk", grad_heads, value_heads, preferred_element_type=jnp.float32
    )
    score_grad = (probs * (prob_grad - delta_sum[..., None]) * HD ** (-0.5)).astype(jnp.bfloat16)
    query_grad = jnp.einsum(
        "hqk,khd->qhd", score_grad, key_heads, preferred_element_type=jnp.float32
    )
    key_grad = jnp.einsum(
        "hqk,qhd->khd", score_grad, query_heads, preferred_element_type=jnp.float32
    )
    count = queries.shape[0]
    return (
        query_grad.reshape(count, H * HD),
        key_grad.reshape(count, H * HD),
        value_grad.reshape(count, H * HD),
    )


def dot_back(left, weight):
    return lax.dot_general(
        left, weight, (((1,), (1,)), ((), ())), preferred_element_type=jnp.float32
    )


def dot_rows(left, right):
    return lax.dot_general(
        left, right, (((0,), (0,)), ((), ())), preferred_element_type=jnp.float32
    )


def on_device(
    layer_in,
    attention_norm_gain,
    attention_norm_bias,
    feedforward_norm_gain,
    feedforward_norm_bias,
    qkv_weight,
    qkv_bias,
    out_weight,
    out_bias,
    fc1_weight,
    fc1_bias,
    fc2_weight,
    fc2_bias,
    cotangent,
):
    half_type = jnp.bfloat16
    complete_sequence = (
        lax.all_gather(attention_norm_gain, "fsdp", axis=0, tiled=True),
        lax.all_gather(attention_norm_bias, "fsdp", axis=0, tiled=True),
        lax.all_gather(feedforward_norm_gain, "fsdp", axis=0, tiled=True),
        lax.all_gather(feedforward_norm_bias, "fsdp", axis=0, tiled=True),
        lax.all_gather(qkv_weight, "fsdp", axis=0, tiled=True),
        lax.all_gather(qkv_bias, "fsdp", axis=0, tiled=True),
        lax.all_gather(out_weight, "fsdp", axis=0, tiled=True),
        lax.all_gather(out_bias, "fsdp", axis=0, tiled=True),
        lax.all_gather(fc1_weight, "fsdp", axis=0, tiled=True),
        lax.all_gather(fc1_bias, "fsdp", axis=0, tiled=True),
        lax.all_gather(fc2_weight, "fsdp", axis=0, tiled=True),
        lax.all_gather(fc2_bias, "fsdp", axis=0, tiled=True),
    )
    incoming_tokens = layer_in[0]
    count = incoming_tokens.shape[0]
    width = incoming_tokens.shape[1]
    cycle_size = lax.axis_size("ctx")
    here_index = lax.axis_index("ctx")
    first_pos = here_index * count
    offsets = jnp.arange(count, dtype=jnp.int32)
    positions = first_pos + offsets
    cos_table, sin_table = angle_tables(positions)
    attention_normed_input, attention_standardized, attention_inverse_spread = layernorm_forward(
        incoming_tokens, complete_sequence[0], complete_sequence[1]
    )
    hidden1 = attention_normed_input.astype(half_type)
    feedforward_normed_input, feedforward_standardized, feedforward_inverse_spread = (
        layernorm_forward(incoming_tokens, complete_sequence[2], complete_sequence[3])
    )
    hidden2 = feedforward_normed_input.astype(half_type)
    projected = jnp.dot(
        hidden1, complete_sequence[4], preferred_element_type=jnp.float32
    ) + complete_sequence[5].astype(jnp.float32)
    queries = (
        rotate_heads(split_heads(projected[:, :width]), cos_table, sin_table)
        .reshape(count, width)
        .astype(half_type)
    )
    keys_local = (
        rotate_heads(split_heads(projected[:, width : 2 * width]), cos_table, sin_table)
        .reshape(count, width)
        .astype(half_type)
    )
    values_local = projected[:, 2 * width :].astype(half_type)
    start_state = (
        jnp.zeros((H, count, HD), jnp.float32),
        jnp.full((H, count), masked_score, jnp.float32),
        jnp.zeros((H, count), jnp.float32),
    )
    key_rows = lax.all_gather(keys_local, "ctx", axis=0, tiled=True)
    value_rows = lax.all_gather(values_local, "ctx", axis=0, tiled=True)
    blocks = key_rows.shape[0] // count
    key_blocks = key_rows.reshape(blocks, count, width)
    value_blocks = value_rows.reshape(blocks, count, width)
    starts = count * jnp.arange(blocks, dtype=jnp.int32)

    def visit(state, item):
        key_block, value_block, key_start = item

        def visit_take(current):
            return merge_state(
                current,
                block_forward(queries, key_block, value_block, positions, key_start + offsets),
            )

        return (lax.cond(key_start <= first_pos, visit_take, lambda current: current, state), None)

    state, unused = lax.scan(visit, start_state, (key_blocks, value_blocks, starts))
    summed, highest, totals = state
    mixed_heads = (
        (summed / totals[..., None]).transpose(1, 0, 2).reshape(count, width).astype(half_type)
    )
    log_totals = highest + jnp.log(totals)
    attn_out = jnp.dot(
        mixed_heads, complete_sequence[6], preferred_element_type=jnp.float32
    ) + complete_sequence[7].astype(jnp.float32)
    pre_act = jnp.dot(
        hidden2, complete_sequence[8], preferred_element_type=jnp.float32
    ) + complete_sequence[9].astype(jnp.float32)
    activation = gelu_value(pre_act).astype(half_type)
    layer_rows = (
        incoming_tokens
        + attn_out
        + jnp.dot(activation, complete_sequence[10], preferred_element_type=jnp.float32)
        + complete_sequence[11].astype(jnp.float32)
    )
    gradient_token_rows = cotangent[0]
    grad_half = gradient_token_rows.astype(half_type)
    grad_mixed = dot_back(grad_half, complete_sequence[6]).astype(half_type)
    delta_sum = jnp.sum(
        split_heads(grad_mixed.astype(jnp.float32) * mixed_heads.astype(jnp.float32)), axis=2
    ).T
    grad_pre = dot_back(grad_half, complete_sequence[10]) * gelu_slope(pre_act)
    grad_pre_half = grad_pre.astype(half_type)
    feedforward_hidden_gradient = dot_back(grad_pre_half, complete_sequence[8])
    blank = jnp.zeros((count, width), jnp.float32)

    def turn_keys(turn_index, state):
        key_rows, value_rows, key_grad, value_grad, query_grad = state
        owner = (here_index + turn_index) % cycle_size
        key_pos = owner * count + offsets

        def turn_take(grads_in):
            parts = block_backward(
                queries, key_rows, value_rows, grad_mixed, log_totals, delta_sum, positions, key_pos
            )
            return (grads_in[0] + parts[0], grads_in[1] + parts[1], grads_in[2] + parts[2])

        query_grad, key_grad, value_grad = lax.cond(
            owner <= here_index,
            turn_take,
            lambda grads_in: grads_in,
            (query_grad, key_grad, value_grad),
        )
        key_rows, value_rows = from_behind((key_rows, value_rows), "ctx", -1)
        key_grad, value_grad = (
            from_behind(key_grad.astype(jnp.bfloat16), "ctx", -1).astype(key_grad.dtype),
            from_behind(value_grad.astype(jnp.bfloat16), "ctx", -1).astype(value_grad.dtype),
        )
        return (key_rows, value_rows, key_grad, value_grad, query_grad)

    final_state = lax.fori_loop(
        0, cycle_size, turn_keys, (keys_local, values_local, blank, blank, blank)
    )
    key_grad_rows, value_grad_rows, query_grad_rows = (
        final_state[2],
        final_state[3],
        final_state[4],
    )
    grad_queries = unrotate_heads(split_heads(query_grad_rows), cos_table, sin_table).reshape(
        count, width
    )
    grad_keys = unrotate_heads(split_heads(key_grad_rows), cos_table, sin_table).reshape(
        count, width
    )
    grad_proj = jnp.concatenate([grad_queries, grad_keys, value_grad_rows], axis=1)
    grad_proj_half = grad_proj.astype(half_type)
    attention_hidden_gradient = dot_back(grad_proj_half, complete_sequence[4])
    input_token_rows = (
        gradient_token_rows
        + layernorm_backward(
            attention_hidden_gradient,
            attention_standardized,
            attention_inverse_spread,
            complete_sequence[0],
        )
        + layernorm_backward(
            feedforward_hidden_gradient,
            feedforward_standardized,
            feedforward_inverse_spread,
            complete_sequence[2],
        )
    )
    out_bias_grad = jnp.sum(gradient_token_rows, axis=0)
    partials = (
        jnp.sum(attention_hidden_gradient * attention_standardized, axis=0),
        jnp.sum(attention_hidden_gradient, axis=0),
        jnp.sum(feedforward_hidden_gradient * feedforward_standardized, axis=0),
        jnp.sum(feedforward_hidden_gradient, axis=0),
        dot_rows(hidden1, grad_proj_half),
        jnp.sum(grad_proj, axis=0),
        dot_rows(mixed_heads, grad_half),
        out_bias_grad,
        dot_rows(hidden2, grad_pre_half),
        jnp.sum(grad_pre, axis=0),
        dot_rows(activation, grad_half),
        out_bias_grad,
    )
    owned = (
        lax.psum_scatter(
            partials[0].astype(jnp.bfloat16), "fsdp", scatter_dimension=0, tiled=True
        ).astype(jnp.float32),
        lax.psum_scatter(
            partials[1].astype(jnp.bfloat16), "fsdp", scatter_dimension=0, tiled=True
        ).astype(jnp.float32),
        lax.psum_scatter(
            partials[2].astype(jnp.bfloat16), "fsdp", scatter_dimension=0, tiled=True
        ).astype(jnp.float32),
        lax.psum_scatter(
            partials[3].astype(jnp.bfloat16), "fsdp", scatter_dimension=0, tiled=True
        ).astype(jnp.float32),
        lax.psum_scatter(
            partials[4].astype(jnp.bfloat16), "fsdp", scatter_dimension=0, tiled=True
        ).astype(jnp.float32),
        lax.psum_scatter(
            partials[5].astype(jnp.bfloat16), "fsdp", scatter_dimension=0, tiled=True
        ).astype(jnp.float32),
        lax.psum_scatter(
            partials[6].astype(jnp.bfloat16), "fsdp", scatter_dimension=0, tiled=True
        ).astype(jnp.float32),
        lax.psum_scatter(
            partials[7].astype(jnp.bfloat16), "fsdp", scatter_dimension=0, tiled=True
        ).astype(jnp.float32),
        lax.psum_scatter(
            partials[8].astype(jnp.bfloat16), "fsdp", scatter_dimension=0, tiled=True
        ).astype(jnp.float32),
        lax.psum_scatter(
            partials[9].astype(jnp.bfloat16), "fsdp", scatter_dimension=0, tiled=True
        ).astype(jnp.float32),
        lax.psum_scatter(
            partials[10].astype(jnp.bfloat16), "fsdp", scatter_dimension=0, tiled=True
        ).astype(jnp.float32),
        lax.psum_scatter(
            partials[11].astype(jnp.bfloat16), "fsdp", scatter_dimension=0, tiled=True
        ).astype(jnp.float32),
    )
    summed_grads = (
        lax.psum(owned[0].astype(jnp.bfloat16), "ctx").astype(jnp.float32),
        lax.psum(owned[1].astype(jnp.bfloat16), "ctx").astype(jnp.float32),
        lax.psum(owned[2].astype(jnp.bfloat16), "ctx").astype(jnp.float32),
        lax.psum(owned[3].astype(jnp.bfloat16), "ctx").astype(jnp.float32),
        lax.psum(owned[4].astype(jnp.bfloat16), "ctx").astype(jnp.float32),
        lax.psum(owned[5].astype(jnp.bfloat16), "ctx").astype(jnp.float32),
        lax.psum(owned[6].astype(jnp.bfloat16), "ctx").astype(jnp.float32),
        lax.psum(owned[7].astype(jnp.bfloat16), "ctx").astype(jnp.float32),
        lax.psum(owned[8].astype(jnp.bfloat16), "ctx").astype(jnp.float32),
        lax.psum(owned[9].astype(jnp.bfloat16), "ctx").astype(jnp.float32),
        lax.psum(owned[10].astype(jnp.bfloat16), "ctx").astype(jnp.float32),
        lax.psum(owned[11].astype(jnp.bfloat16), "ctx").astype(jnp.float32),
    )
    return (
        layer_rows[None],
        input_token_rows[None],
        summed_grads[0],
        summed_grads[1],
        summed_grads[2],
        summed_grads[3],
        summed_grads[4],
        summed_grads[5],
        summed_grads[6],
        summed_grads[7],
        summed_grads[8],
        summed_grads[9],
        summed_grads[10],
        summed_grads[11],
    )


def solution(mesh):
    return jax.shard_map(
        on_device,
        mesh=mesh,
        in_specs=(
            P("fsdp", "ctx", None),
            P("fsdp"),
            P("fsdp"),
            P("fsdp"),
            P("fsdp"),
            P("fsdp", None),
            P("fsdp"),
            P("fsdp", None),
            P("fsdp"),
            P("fsdp", None),
            P("fsdp"),
            P("fsdp", None),
            P("fsdp"),
            P("fsdp", "ctx", None),
        ),
        out_specs=(
            P("fsdp", "ctx", None),
            P("fsdp", "ctx", None),
            P("fsdp"),
            P("fsdp"),
            P("fsdp"),
            P("fsdp"),
            P("fsdp", None),
            P("fsdp"),
            P("fsdp", None),
            P("fsdp"),
            P("fsdp", None),
            P("fsdp"),
            P("fsdp", None),
            P("fsdp"),
        ),
        check_vma=False,
    )
```

profile of v0, /device:TPU:0, one launch (start us, length us, event | category | flops | bytes accessed | tf_op | source)
XLA Modules:
  0.0 1117.4 jit_solution(5110623383960042034)
XLA Ops:
  8.7 14.8 %all-gather.2 = bf16[4,1,768]{2,1,0:T(2,128)(2,1)S(1)} all-gather(bf16[1,1,768]{2,1,0:T(2,128)(2,1)S(1)} %reshape.276), channel_id=1, replica_groups=mesh['ctx'=8,'fsdp'=4] {'fsdp'}, dimensions={0}, use_global_device_ids=true | all-gather | bytes 7680 | tf_op jit(solution)/shard_map/all_gather | solution.py:197
  24.2 12.4 %all-gather.1 = bf16[4,1,256]{2,1,0:T(2,128)(2,1)S(1)} all-gather(bf16[1,1,256]{2,1,0:T(2,128)(2,1)S(1)} %reshape.274), channel_id=1, replica_groups=mesh['ctx'=8,'fsdp'=4] {'fsdp'}, dimensions={0}, use_global_device_ids=true | all-gather | bytes 2560 | tf_op jit(solution)/shard_map/all_gather | solution.py:193
  37.3 8.0 all-gather
  46.8 80.9 %all-gather.14.cloned.1.call-done = bf16[1024,3072]{1,0:T(8,128)(2,1)} async-done(((bf16[256,3072]{1,0:T(8,128)(2,1)}), bf16[1024,3072]{1,0:T(8,128)(2,1)}) %all-gather.14.cloned.1.call-update) | async-done | bytes 6291472 | tf_op jit(solution)/shard_map/all_gather | solution.py:196
  127.8 3.8 convolution_add_fusion.1
  140.1 23.4 %all-gather.16.cloned.1.call-done = bf16[1024,1024]{1,0:T(8,128)(2,1)} async-done(((bf16[128,1024]{1,0:T(8,128)(2,1)}), bf16[1024,1024]{1,0:T(8,128)(2,1)}) %all-gather.16.cloned.1.call-update) | async-done | bytes 2097168 | tf_op jit(solution)/shard_map/all_gather | solution.py:241
  163.5 3.9 copy.61
  167.4 26.4 %all-gather.18.cloned.1.call-done = bf16[1024,1024]{1,0:T(8,128)(2,1)} async-done(((bf16[128,1024]{1,0:T(8,128)(2,1)}), bf16[1024,1024]{1,0:T(8,128)(2,1)}) %all-gather.18.cloned.1.call-update) | async-done | bytes 2097168 | tf_op jit(solution)/shard_map/all_gather | solution.py:242
  193.8 3.9 copy.62
  197.8 13.1 %while.41 = (s32[]{:T(128)}, f32[16,128,64]{1,2,0:T(8,128)S(1)}, f32[16,128]{1,0:T(8,128)S(1)}, f32[16,128]{1,0:T(8,128)S(1)}, s32[8]{0:T(128)S(1)}, /*index=5*/...) while((s32[]{:T(128)}, f32[16,128,64]{1,2,0:T(8,128)S(1)}, ...), condition=%wide.region_7.8_spmd.clone.clone, body=%wide.region_2.7_spmd.clone.clone.sunk | while | flops 69886208 | bytes 6213411 | solution.py:259
  199.0 2.8 conditional.8
  213.4 27.5 %all-gather.20.cloned.1.call-done = bf16[1024,1024]{1,0:T(8,128)(2,1)} async-done(((bf16[256,1024]{1,0:T(8,128)(2,1)}), bf16[1024,1024]{1,0:T(8,128)(2,1)}) %all-gather.20.cloned.1.call-update) | async-done | bytes 2097168 | tf_op jit(solution)/shard_map/all_gather | solution.py:198
  240.9 3.1 convert_multiply_fusion
  246.2 152.6 %while.40 = (s32[]{:T(128)}, bf16[128,1024]{0,1:T(8,128)(2,1)S(1)}, bf16[128,1024]{0,1:T(8,128)(2,1)S(1)}, f32[128,1024]{0,1:T(8,128)}, f32[128,1024]{0,1:T(8,12...) while((s32[]{:T(128)}, bf16[128,1024]{0,1:T(8,128)(2,1)S(1)}, ...), condition=%wide.region_12.13_spmd.clone, body=%wide.region_9.12_spmd.clone.sunk | while | flops 171327760 | bytes 27578544 | solution.py:313
  257.5 2.8 collective-permute-done
  260.2 2.8 collective-permute-done.1
  264.3 5.8 collective-permute-start.2
  270.4 3.7 collective-permute-done.2
  276.9 2.8 collective-permute-done
  279.6 2.8 collective-permute-done.1
  283.7 5.8 collective-permute-start.2
  289.8 3.7 collective-permute-done.2
  296.3 2.8 collective-permute-done
  299.0 2.8 collective-permute-done.1
  303.1 5.8 collective-permute-start.2
  309.2 3.7 collective-permute-done.2
  315.7 2.8 collective-permute-done
  318.4 2.8 collective-permute-done.1
  322.5 5.8 collective-permute-start.2
  328.6 3.7 collective-permute-done.2
  335.1 2.8 collective-permute-done
  337.8 2.8 collective-permute-done.1
  341.9 5.8 collective-permute-start.2
  348.0 3.7 collective-permute-done.2
  354.5 2.8 collective-permute-done
  357.2 2.8 collective-permute-done.1
  361.3 5.8 collective-permute-start.2
  367.4 3.7 collective-permute-done.2
  373.9 2.8 collective-permute-done
  376.6 2.8 collective-permute-done.1
  380.7 5.8 collective-permute-start.2
  386.8 3.7 collective-permute-done.2
  393.3 2.8 collective-permute-done
  396.0 2.8 collective-permute-done.1
  403.1 4.5 convolution_convert_fusion.2
  408.3 12.5 %all_gather.53 = bf16[4096]{0:T(1024)(128)(2,1)S(1)} all-gather(bf16[1024]{0:T(1024)(128)(2,1)S(1)} %copy-done.23), channel_id=1, replica_groups=mesh['ctx'=8,'fsdp'=4] {'fsdp'}, dimensions={0}, use_global_device_ids=true | all-gather | bytes 10240 | tf_op jit(solution)/shard_map/all_gather | solution.py:201
  420.9 15.0 %all-gather.5 = bf16[4,1,256]{2,1,0:T(2,128)(2,1)S(1)} all-gather(bf16[1,1,256]{2,1,0:T(2,128)(2,1)S(1)} %reshape.282), channel_id=1, replica_groups=mesh['ctx'=8,'fsdp'=4] {'fsdp'}, dimensions={0}, use_global_device_ids=true | all-gather | bytes 2560 | tf_op jit(solution)/shard_map/all_gather | solution.py:195
  435.8 11.4 %all-gather.4 = bf16[4,1,256]{2,1,0:T(2,128)(2,1)S(1)} all-gather(bf16[1,1,256]{2,1,0:T(2,128)(2,1)S(1)} %reshape.280), channel_id=1, replica_groups=mesh['ctx'=8,'fsdp'=4] {'fsdp'}, dimensions={0}, use_global_device_ids=true | all-gather | bytes 2560 | tf_op jit(solution)/shard_map/all_gather | solution.py:194
  447.2 4.7 convolution_add_fusion
  452.0 88.3 %all-gather.24.cloned.1.call-done = bf16[4096,1024]{1,0:T(8,128)(2,1)} async-done(((bf16[1024,1024]{1,0:T(8,128)(2,1)}), bf16[4096,1024]{1,0:T(8,128)(2,1)}) %all-gather.24.cloned.1.call-update) | async-done | bytes 8388624 | tf_op jit(solution)/shard_map/all_gather | solution.py:202
  540.3 6.7 fusion.58
  547.9 5.7 convolution_convert_fusion.1
  553.7 5.6 convolution_convert_fusion
  560.5 8.4 all-gather.6
  568.9 10.9 all-gather.3
  585.1 112.3 %reduce-scatter.5.cloned.1.call-done = bf16[256,3072]{1,0:T(8,128)(2,1)} async-done(((bf16[1024,3072]{1,0:T(8,128)(2,1)}), bf16[256,3072]{1,0:T(8,128)(2,1)}) %reduce-scatter.5.cloned.1.call-update) | async-done | bytes 1572880 | tf_op jit(solution)/shard_map/reduce_scatter | solution.py:373
  697.4 147.5 %reduce-scatter.9.cloned.1.call-done = bf16[256,4096]{1,0:T(8,128)(2,1)} async-done(((bf16[1024,4096]{1,0:T(8,128)(2,1)}), bf16[256,4096]{1,0:T(8,128)(2,1)}) %reduce-scatter.9.cloned.1.call-update) | async-done | bytes 2097168 | tf_op jit(solution)/shard_map/reduce_scatter | solution.py:385
  844.9 147.5 %reduce-scatter.11.cloned.1.call-done = bf16[1024,1024]{1,0:T(8,128)(2,1)} async-done(((bf16[4096,1024]{1,0:T(8,128)(2,1)}), bf16[1024,1024]{1,0:T(8,128)(2,1)}) %reduce-scatter.11.cloned.1.call-update) | async-done | bytes 2097168 | tf_op jit(solution)/shard_map/reduce_scatter | solution.py:391
  992.4 6.3 fusion.52
  1001.5 8.2 multiply_reduce_fusion
  1009.7 18.9 %all-reduce.9 = (bf16[1024]{0:T(1024)(128)(2,1)S(1)}, bf16[1024]{0:T(1024)(128)(2,1)S(1)}, bf16[1024]{0:T(1024)(128)(2,1)S(1)}, bf16[1024]{0:T(1024)(128)(2,1)S(...) all-reduce(bf16[1024]{0:T(1024)(128)(2,1)S(1)} %get-tuple-element.7, ...), channel_id=2, replica_groups=mesh['ctx'=8,'fsdp'=4] {'fsdp'}, use_global_device_ids=true, to_apply=%region_18.19.clone | all-reduce | flops 12288 | bytes 49152
  1029.1 12.4 %all-reduce.7 = (bf16[256]{0:T(256)(128)(2,1)S(1)}, bf16[256]{0:T(256)(128)(2,1)S(1)}, bf16[256]{0:T(256)(128)(2,1)S(1)}, bf16[256]{0:T(256)(128)(2,1)S(1)}, bf1...) all-reduce(bf16[256]{0:T(256)(128)(2,1)S(1)} %dynamic-slice.1, ...), channel_id=1, replica_groups=mesh['ctx'=8,'fsdp'=4] {'ctx'}, use_global_device_ids=true, to_apply=%region_19.20 | all-reduce | flops 3072 | bytes 12288 | tf_op jit(solution)/shard_map/psum | solution.py:399
  1048.4 52.3 %all-reduce.12.cloned.1.call-done = (bf16[256,3072]{1,0:T(8,128)(2,1)}, bf16[256,1024]{1,0:T(8,128)(2,1)}, bf16[256,4096]{1,0:T(8,128)(2,1)}, bf16[1024,1024]{1,0:T(8,128)(2,1)}) async-done(((bf16[256,3072]{1,0:T(8,128)(2,1)}, bf16[256,1024]{1,0:T(8,128)(2,1)}, bf16[256,4096]{1,0:T(8,128)(2,1)}, bf16[1024,1024]{1,0:T(8,128)(2,1)}), (bf16[256,3072]{1,0:T(8,128)(2,1)}, bf16[256,1024]{1,0:T(8,128)(2,1)}, ...) | async-done | bytes 6291472 | tf_op jit(solution)/shard_map/psum | solution.py:403
  1100.7 3.6 convert_element_type.275
  (314 shorter events, 95.7 us)
Async XLA Ops:
  7.2 39.3 %copy-start = (f32[1,128,1024]{2,1,0:T(8,128)S(1)}, f32[1,128,1024]{2,1,0:T(8,128)}, u32[]{:S(2)}) copy-start(f32[1,128,1024]{2,1,0:T(8,128)} %param.22) | copy-start | bytes 1572868
  7.2 120.6 %all-gather.14.cloned.1.call-start = ((), (), s32[]{:S(2)}) async-start(), calls=%async_computation.4 | async-start | bytes 7864320 | tf_op jit(solution)/shard_map/all_gather | solution.py:196
  7.9 155.6 %all-gather.16.cloned.1.call-start = ((), (), s32[]{:S(2)}) async-start(), calls=%async_computation.5 | async-start | bytes 2359296 | tf_op jit(solution)/shard_map/all_gather | solution.py:241
  137.4 56.4 %all-gather.18.cloned.1.call-start = ((), (), s32[]{:S(2)}) async-start(), calls=%async_computation.6 | async-start | bytes 2359296 | tf_op jit(solution)/shard_map/all_gather | solution.py:242
  138.2 102.7 %all-gather.20.cloned.1.call-start = ((), (), s32[]{:S(2)}) async-start(), calls=%async_computation.7 | async-start | bytes 2621440 | tf_op jit(solution)/shard_map/all_gather | solution.py:198
  138.8 308.5 %all-gather.22.cloned.1.call-start = ((), (), s32[]{:S(2)}) async-start(), calls=%async_computation.8 | async-start | bytes 10485760 | tf_op jit(solution)/shard_map/all_gather | solution.py:200
  139.4 400.9 %all-gather.24.cloned.1.call-start = ((), (), s32[]{:S(2)}) async-start(), calls=%async_computation.9 | async-start | bytes 10485760 | tf_op jit(solution)/shard_map/all_gather | solution.py:202
  139.9 445.1 %reduce-scatter.7.cloned.1.call-start = ((), (), s32[]{:S(2)}) async-start(), calls=%async_computation.11 | async-start | bytes 2621440 | tf_op jit(solution)/shard_map/reduce_scatter | solution.py:379
  197.8 13.2 %copy-start.4 = (f32[1,128,1024]{2,1,0:T(8,128)S(1)}, f32[1,128,1024]{2,1,0:T(8,128)}, u32[]{:S(2)}) copy-start(f32[1,128,1024]{2,1,0:T(8,128)} %param.35) | copy-start | bytes 1572868
  213.0 484.4 %reduce-scatter.5.cloned.1.call-start = ((), (), s32[]{:S(2)}) async-start(), calls=%async_computation.10 | async-start | bytes 7864320 | tf_op jit(solution)/shard_map/reduce_scatter | solution.py:373
  249.1 5.5 collective-permute-start.2
  250.8 6.7 collective-permute-start.3
  251.7 8.5 collective-permute-start
  251.8 11.3 %collective-permute-start.1 = (bf16[128,1024]{0,1:T(8,128)(2,1)S(1)}, bf16[128,1024]{0,1:T(8,128)(2,1)S(1)}, u32[]{:S(2)}, u32[]{:S(2)}) collective-permute-start(bf16[128,1024]{0,1:T(8,128)(2,1)S(1)} %copy.100), channel_id=1, source_target_pairs={{0,28},{4,0},{8,4},{12,8},{16,12},{20,16},{24,20},{28,24},{1,29},{... | collective-permute-start | bytes 786440 | tf_op jit(solution)/shard_map/while/body/eval_jaxpr/ppermute | solution.py:21
  264.3 9.7 collective-permute-start.2
  270.2 6.7 collective-permute-start.3
  270.2 9.4 collective-permute-start
  270.3 12.1 %collective-permute-start.1 = (bf16[128,1024]{0,1:T(8,128)(2,1)S(1)}, bf16[128,1024]{0,1:T(8,128)(2,1)S(1)}, u32[]{:S(2)}, u32[]{:S(2)}) collective-permute-start(bf16[128,1024]{0,1:T(8,128)(2,1)S(1)} %copy.100), channel_id=1, source_target_pairs={{0,28},{4,0},{8,4},{12,8},{16,12},{20,16},{24,20},{28,24},{1,29},{... | collective-permute-start | bytes 786440 | tf_op jit(solution)/shard_map/while/body/eval_jaxpr/ppermute | solution.py:21
  283.7 9.7 collective-permute-start.2
  289.6 6.7 collective-permute-start.3
  289.6 9.4 collective-permute-start
  289.7 12.1 %collective-permute-start.1 = (bf16[128,1024]{0,1:T(8,128)(2,1)S(1)}, bf16[128,1024]{0,1:T(8,128)(2,1)S(1)}, u32[]{:S(2)}, u32[]{:S(2)}) collective-permute-start(bf16[128,1024]{0,1:T(8,128)(2,1)S(1)} %copy.100), channel_id=1, source_target_pairs={{0,28},{4,0},{8,4},{12,8},{16,12},{20,16},{24,20},{28,24},{1,29},{... | collective-permute-start | bytes 786440 | tf_op jit(solution)/shard_map/while/body/eval_jaxpr/ppermute | solution.py:21
  303.1 9.7 collective-permute-start.2
  309.0 6.7 collective-permute-start.3
  309.0 9.4 collective-permute-start
  309.1 12.1 %collective-permute-start.1 = (bf16[128,1024]{0,1:T(8,128)(2,1)S(1)}, bf16[128,1024]{0,1:T(8,128)(2,1)S(1)}, u32[]{:S(2)}, u32[]{:S(2)}) collective-permute-start(bf16[128,1024]{0,1:T(8,128)(2,1)S(1)} %copy.100), channel_id=1, source_target_pairs={{0,28},{4,0},{8,4},{12,8},{16,12},{20,16},{24,20},{28,24},{1,29},{... | collective-permute-start | bytes 786440 | tf_op jit(solution)/shard_map/while/body/eval_jaxpr/ppermute | solution.py:21
  322.5 9.7 collective-permute-start.2
  328.4 6.7 collective-permute-start.3
  328.4 9.4 collective-permute-start
  328.5 12.1 %collective-permute-start.1 = (bf16[128,1024]{0,1:T(8,128)(2,1)S(1)}, bf16[128,1024]{0,1:T(8,128)(2,1)S(1)}, u32[]{:S(2)}, u32[]{:S(2)}) collective-permute-start(bf16[128,1024]{0,1:T(8,128)(2,1)S(1)} %copy.100), channel_id=1, source_target_pairs={{0,28},{4,0},{8,4},{12,8},{16,12},{20,16},{24,20},{28,24},{1,29},{... | collective-permute-start | bytes 786440 | tf_op jit(solution)/shard_map/while/body/eval_jaxpr/ppermute | solution.py:21
  341.9 9.7 collective-permute-start.2
  347.8 6.7 collective-permute-start.3
  347.8 9.4 collective-permute-start
  347.9 12.1 %collective-permute-start.1 = (bf16[128,1024]{0,1:T(8,128)(2,1)S(1)}, bf16[128,1024]{0,1:T(8,128)(2,1)S(1)}, u32[]{:S(2)}, u32[]{:S(2)}) collective-permute-start(bf16[128,1024]{0,1:T(8,128)(2,1)S(1)} %copy.100), channel_id=1, source_target_pairs={{0,28},{4,0},{8,4},{12,8},{16,12},{20,16},{24,20},{28,24},{1,29},{... | collective-permute-start | bytes 786440 | tf_op jit(solution)/shard_map/while/body/eval_jaxpr/ppermute | solution.py:21
  361.3 9.7 collective-permute-start.2
  367.2 6.7 collective-permute-start.3
  367.2 9.4 collective-permute-start
  367.3 12.1 %collective-permute-start.1 = (bf16[128,1024]{0,1:T(8,128)(2,1)S(1)}, bf16[128,1024]{0,1:T(8,128)(2,1)S(1)}, u32[]{:S(2)}, u32[]{:S(2)}) collective-permute-start(bf16[128,1024]{0,1:T(8,128)(2,1)S(1)} %copy.100), channel_id=1, source_target_pairs={{0,28},{4,0},{8,4},{12,8},{16,12},{20,16},{24,20},{28,24},{1,29},{... | collective-permute-start | bytes 786440 | tf_op jit(solution)/shard_map/while/body/eval_jaxpr/ppermute | solution.py:21
  380.7 9.7 collective-permute-start.2
  386.6 6.7 collective-permute-start.3
  386.6 9.4 collective-permute-start
  386.7 12.1 %collective-permute-start.1 = (bf16[128,1024]{0,1:T(8,128)(2,1)S(1)}, bf16[128,1024]{0,1:T(8,128)(2,1)S(1)}, u32[]{:S(2)}, u32[]{:S(2)}) collective-permute-start(bf16[128,1024]{0,1:T(8,128)(2,1)S(1)} %copy.100), channel_id=1, source_target_pairs={{0,28},{4,0},{8,4},{12,8},{16,12},{20,16},{24,20},{28,24},{1,29},{... | collective-permute-start | bytes 786440 | tf_op jit(solution)/shard_map/while/body/eval_jaxpr/ppermute | solution.py:21
  407.7 13.2 %copy-start.25 = (bf16[256]{0:T(256)(128)(2,1)S(1)}, bf16[256]{0:T(256)(128)(2,1)}, u32[]{:S(2)}) copy-start(bf16[256]{0:T(256)(128)(2,1)} %param.26) | copy-start | bytes 1540
  407.7 28.2 %copy-start.26 = (bf16[256]{0:T(256)(128)(2,1)S(1)}, bf16[256]{0:T(256)(128)(2,1)}, u32[]{:S(2)}) copy-start(bf16[256]{0:T(256)(128)(2,1)} %param.25) | copy-start | bytes 1540
  407.7 437.2 %reduce-scatter.9.cloned.1.call-start = ((), (), s32[]{:S(2)}) async-start(), calls=%async_computation.12 | async-start | bytes 10485760 | tf_op jit(solution)/shard_map/reduce_scatter | solution.py:385
  452.0 101.8 %copy-start.1 = (f32[128,4096]{1,0:T(8,128)}, f32[128,4096]{1,0:T(8,128)S(1)}, u32[]{:S(2)}) copy-start(f32[128,4096]{1,0:T(8,128)S(1)} %convolution_add_fusion) | copy-start | bytes 6291460
  553.7 438.7 %reduce-scatter.11.cloned.1.call-start = ((), (), s32[]{:S(2)}) async-start(), calls=%async_computation.13 | async-start | bytes 10485760 | tf_op jit(solution)/shard_map/reduce_scatter | solution.py:391
  559.4 9.5 copy-start.28
  559.4 20.4 %copy-start.29 = (u32[32]{0:T(128)S(1)}, u32[32]{0:T(128)}, u32[]{:S(2)}) copy-start(u32[32]{0:T(128)} %constant.139) | copy-start | bytes 388
  559.4 541.2 %all-reduce.12.cloned.1.call-start = ((), (), s32[]{:S(2)}) async-start(), calls=%async_computation.14 | async-start | bytes 12582912 | tf_op jit(solution)/shard_map/psum | solution.py:403
  992.4 6.9 slice-start
  992.4 6.3 copy-start.8
  992.4 6.3 copy-start.10
  992.4 6.8 slice-start.1
  1001.5 8.2 copy-start.12
  1001.5 43.4 %copy-start.11 = (bf16[1024,1024]{1,0:T(8,128)(2,1)S(1)}, bf16[1024,1024]{1,0:T(8,128)(2,1)}, u32[]{:S(2)}) copy-start(bf16[1024,1024]{1,0:T(8,128)(2,1)} %all-gather.20.cloned.1.call-done) | copy-start | bytes 6291460
  1001.5 43.4 %copy-start.17 = (bf16[16,128,64]{1,2,0:T(8,128)(2,1)S(1)}, bf16[16,128,64]{1,2,0:T(8,128)(2,1)}, u32[]{:S(2)}) copy-start(bf16[16,128,64]{1,2,0:T(8,128)(2,1)} %copy-done.16) | copy-start | bytes 786436
  1009.7 37.6 %copy-start.6 = (f32[1,128,1024]{2,1,0:T(8,128)S(1)}, f32[1,128,1024]{2,1,0:T(8,128)}, u32[]{:S(2)}) copy-start(f32[1,128,1024]{2,1,0:T(8,128)} %param.35) | copy-start | bytes 1572868
  1041.4 5.8 copy-start.13
  1041.4 5.8 copy-start.21
  1044.3 66.0 %copy-start.24 = (f32[256]{0:T(256)}, f32[256]{0:T(256)S(1)}, u32[]{:S(2)}) copy-start(f32[256]{0:T(256)S(1)} %convert_element_type.283) | copy-start | bytes 3076
  1100.7 3.6 copy-start.22
  1100.7 4.7 copy-start.20
  1105.3 2.5 copy-start.19
  (11 other events, 14.2 us)
Sparse Core Ops, SparseCore 0:
  9.6 118.1 all-gather.13
  137.5 25.9 all-gather.15
  166.0 27.7 all-gather.17
  195.2 45.6 all-gather.19
  242.3 148.4 all-gather.21
  392.2 148.0 all-gather.23
  543.1 41.8 reduce-scatter.6
  587.4 109.9 reduce-scatter.4
  699.7 145.1 reduce-scatter.8
  847.1 145.2 reduce-scatter.10
  996.0 104.6 all-reduce.11
where the time goes:
time: 1120 us
  waiting for transfers between devices  799 us (71%)
  blocking collectives  125 us (11%)
  matrix products  58 us (5%)
  starting transfers between devices  45.8 us (4%)
  other arithmetic  36 us (3%)
  local copies, waits for them, and re-layouts  30.6 us (3%)
  between operations  16.4 us (1%)
    reduce_scatter x1, waiting for transfers between devices, on_device(): lax.psum_scatter(partials[8].astype(jnp.bfloat16), 'fsdp', scatter_dimens...  148 us
    reduce_scatter x1, waiting for transfers between devices, on_device(): lax.psum_scatter(partials[10].astype(jnp.bfloat16), 'fsdp', scatter_dimen...  147 us
    reduce_scatter x1, waiting for transfers between devices, on_device(): lax.psum_scatter(partials[4].astype(jnp.bfloat16), 'fsdp', scatter_dimens...  112 us
    ppermute x32, waiting for transfers between devices, from_behind(): lax.ppermute(array, axis, [(i, (i + by) % devices) for i in range(devices)])  88.3 us
    all_gather x1, waiting for transfers between devices, on_device(): lax.all_gather(fc2_weight, 'fsdp', axis=0, tiled=True)  88.3 us
    all_gather x1, waiting for transfers between devices, on_device(): lax.all_gather(qkv_weight, 'fsdp', axis=0, tiled=True)  80.9 us
    psum x1, waiting for transfers between devices, on_device(): lax.psum(owned[4].astype(jnp.bfloat16), 'ctx').astype(jnp.float32)  52.3 us
    ppermute x32, starting transfers between devices, from_behind(): lax.ppermute(array, axis, [(i, (i + by) % devices) for i in range(devices)])  45.4 us
  transfers between devices with their start and end apart: 43, of which 42 were waited for; matrix products, arithmetic and copies ran while one was open for 9% of the time, Pallas kernels for 0%

commit v1 on v0

v1 whole, which is shorter than its diff:
```python
import functools
import math

import jax
import jax.numpy as jnp
from jax import lax
from jax.experimental import pallas as pl
from jax.experimental.pallas import tpu as pltpu
from jax.sharding import PartitionSpec as P

H = 16
HD = 64
ROT = 16

norm_eps = 1e-05
masked_score = -1e30
root_half = 1.0 / math.sqrt(2.0)
root_two_pi = 1.0 / math.sqrt(2.0 * math.pi)
BF = jnp.bfloat16
F32 = jnp.float32
MESH = pl.DeviceIdType.MESH
VM = pl.BlockSpec(memory_space=pltpu.VMEM)


class Group:
    def __init__(self, name, F, C):
        self.name = name
        self.f = lax.axis_index("fsdp")
        self.c = lax.axis_index("ctx")
        if name == "fsdp":
            self.n, self.me = F, self.f
        elif name == "ctx":
            self.n, self.me = C, self.c
        elif name == "plane":
            self.n, self.me = C // 2, self.c // 2
        else:
            self.n, self.me = 2, lax.rem(self.c, 2)

    def peer(self, k):
        return lax.rem(self.me + k, self.n)

    def device(self, index):
        if self.name == "fsdp":
            return {"fsdp": index}
        if self.name == "ctx":
            return {"ctx": index}
        if self.name == "plane":
            return {"ctx": index * 2 + lax.rem(self.c, 2)}
        return {"ctx": (self.c // 2) * 2 + index}


GROUP_SIZE = {
    "fsdp": lambda F, C: F,
    "ctx": lambda F, C: C,
    "plane": lambda F, C: C // 2,
    "core": lambda F, C: 2,
}


def comm(cid, F, C, inputs, outputs, scratch, ops):
    names = list(inputs) + list(outputs) + list(scratch)
    sizes = [GROUP_SIZE[op[0]](F, C) for op in ops]
    offset = [sum(sizes[:i]) for i in range(len(ops))]
    total = sum(sizes)
    used = sorted({op[0] for op in ops})

    def kernel(*args):
        refs = dict(zip(names, args))
        send_sem, recv_sem = args[len(names)], args[len(names) + 1]
        groups = {u: Group(u, F, C) for u in used}
        barrier = pltpu.get_barrier_semaphore()
        count = 0
        for u in used:
            if u in ("plane", "core") and "ctx" in used:
                continue
            g = groups[u]
            for k in range(1, g.n):
                pl.semaphore_signal(
                    barrier, inc=1, device_id=g.device(g.peer(k)), device_id_type=MESH
                )
                count += 1
        pl.semaphore_wait(barrier, count)
        started = {}
        done = set()

        def finish(i):
            if i in done:
                return
            done.add(i)
            for copy in started[i]:
                copy.wait()

        for i, (gname, src_view, dst_view, own, after) in enumerate(ops):
            for j in after:
                finish(j)
            g = groups[gname]
            copies = []
            for k in range(1, g.n):
                peer = g.peer(k)
                copy = pltpu.make_async_remote_copy(
                    src_ref=src_view(refs, g, peer),
                    dst_ref=dst_view(refs, g),
                    send_sem=send_sem.at[offset[i] + k],
                    recv_sem=recv_sem.at[offset[i] + k],
                    device_id=g.device(peer),
                    device_id_type=MESH,
                )
                copy.start()
                copies.append(copy)
            if own:
                copy = pltpu.make_async_copy(
                    src_view(refs, g, g.me), dst_view(refs, g), send_sem.at[offset[i]]
                )
                copy.start()
                copies.append(copy)
            started[i] = copies
        for i in range(len(ops)):
            finish(i)

    result = pl.pallas_call(
        kernel,
        name="comm%d" % cid,
        out_shape=[jax.ShapeDtypeStruct(s, d) for s, d in outputs.values()],
        in_specs=[VM] * len(inputs),
        out_specs=[VM] * len(outputs),
        scratch_shapes=[pltpu.VMEM(s, d) for s, d in scratch.values()]
        + [pltpu.SemaphoreType.DMA((total,)), pltpu.SemaphoreType.DMA((total,))],
        compiler_params=pltpu.CompilerParams(
            collective_id=cid, has_side_effects=True, vmem_limit_bytes=60 * 2**20
        ),
    )(*inputs.values())
    return dict(zip(outputs, result))


def op_all_to_all(group, src, dst, after=()):
    return (group, lambda r, g, p: r[src].at[p], lambda r, g: r[dst].at[g.me], True, after)


def op_gather(group, src, dst, after=()):
    return (group, lambda r, g, p: r[src], lambda r, g: r[dst].at[g.me], True, after)


def attention_kernel(in_ref, cos_ref, sa_ref, sb_ref, out_ref, dk_ref, dv_ref, dq_ref):
    length, CH = in_ref.shape[1:]
    rows = min(256, length)
    dk_ref[...] = jnp.zeros_like(dk_ref)
    dv_ref[...] = jnp.zeros_like(dv_ref)
    lane = lax.broadcasted_iota(jnp.int32, (rows, CH), 1)
    masks = [(lane >= h * HD) & (lane < (h + 1) * HD) for h in range(CH // HD)]

    def nt(a, b):
        return lax.dot_general(a, b, (((1,), (1,)), ((), ())), preferred_element_type=F32)

    def tn(a, b):
        return lax.dot_general(a, b, (((0,), (0,)), ((), ())), preferred_element_type=F32)

    for i in range(length // rows):
        lo, hi = i * rows, (i + 1) * rows
        q = in_ref[0, lo:hi, :] * jnp.asarray(HD**-0.5, BF)
        g = in_ref[3, lo:hi, :]
        k = in_ref[1, :hi, :]
        v = in_ref[2, :hi, :]
        visible = lo + lax.broadcasted_iota(
            jnp.int32, (rows, hi), 0
        ) >= lax.broadcasted_iota(jnp.int32, (rows, hi), 1)
        mixed = None
        dq = None
        for h in range(CH // HD):
            qm = jnp.where(masks[h], q, jnp.zeros_like(q))
            gm = jnp.where(masks[h], g, jnp.zeros_like(g))
            s = jnp.where(visible, nt(qm, k), masked_score)
            p = jnp.exp(s - jnp.max(s, axis=1, keepdims=True))
            inv = 1.0 / jnp.sum(p, axis=1, keepdims=True)
            o = (jnp.dot(p.astype(BF), v, preferred_element_type=F32) * inv).astype(BF)
            delta = jnp.sum(gm.astype(F32) * o.astype(F32), axis=1, keepdims=True)
            probs = p * inv
            dv_ref[:hi, :] += tn(probs.astype(BF), gm)
            ds = (probs * (nt(gm, v) - delta)).astype(BF)
            dk_ref[:hi, :] += tn(ds, qm)
            dqh = jnp.dot(ds, k, preferred_element_type=F32)
            mixed = o if h == 0 else jnp.where(masks[h], o, mixed)
            dq = dqh if h == 0 else jnp.where(masks[h], dqh, dq)
        out_ref[0, lo:hi, :] = mixed
        dq_ref[lo:hi, :] = dq * HD**-0.5

    def unrotate(x):
        left = pltpu.roll(x, CH - ROT // 2, 1)
        right = pltpu.roll(x, ROT // 2, 1)
        return x * cos_ref[...] - left * sa_ref[...] - right * sb_ref[...]

    out_ref[1] = unrotate(dq_ref[...]).astype(BF)
    out_ref[2] = unrotate(dk_ref[...]).astype(BF)
    out_ref[3] = dv_ref[...].astype(BF)


def attention(stack, tables):
    length, CH = stack.shape[1:]
    return pl.pallas_call(
        attention_kernel,
        name="attention",
        out_shape=jax.ShapeDtypeStruct((4, length, CH), BF),
        in_specs=[VM] * 4,
        out_specs=VM,
        scratch_shapes=[pltpu.VMEM((length, CH), F32)] * 3,
        compiler_params=pltpu.CompilerParams(vmem_limit_bytes=60 * 2**20),
    )(stack, *tables)


def rotary_tables(positions, width):
    half = ROT // 2
    freqs = jnp.power(10000.0, -2.0 * jnp.arange(half, dtype=F32) / ROT)
    angles = positions.astype(F32)[:, None] * freqs[None, :]
    c, s = jnp.cos(angles), jnp.sin(angles)
    n = positions.shape[0]
    rest = HD - ROT
    zero = jnp.zeros((n, half), F32)
    cos_t = jnp.concatenate([c, c, jnp.ones((n, rest), F32)], axis=1)
    sa = jnp.concatenate([-s, zero, jnp.zeros((n, rest), F32)], axis=1)
    sb = jnp.concatenate([zero, s, jnp.zeros((n, rest), F32)], axis=1)
    return tuple(jnp.tile(t, (1, width // HD)) for t in (cos_t, sa, sb))


def dot(a, b):
    return jnp.dot(a, b, preferred_element_type=F32)


def dot_nt(a, b):
    return lax.dot_general(a, b, (((1,), (1,)), ((), ())), preferred_element_type=F32)


def dot_tn(a, b):
    return lax.dot_general(a, b, (((0,), (0,)), ((), ())), preferred_element_type=F32)


def on_device(
    F,
    C,
    layer_in,
    ln1_gain,
    ln1_bias,
    ln2_gain,
    ln2_bias,
    qkv_weight,
    qkv_bias,
    out_weight,
    out_bias,
    fc1_weight,
    fc1_bias,
    fc2_weight,
    fc2_bias,
    cotangent,
):
    x = layer_in[0]
    cot = cotangent[0]
    T, D = x.shape
    FF = fc1_weight.shape[1]
    DF, FFF = D // F, FF // F
    R = D // (F * C)
    RF = FF // (F * C)
    PN = C // 2
    f_index = lax.axis_index("fsdp")
    c_index = lax.axis_index("ctx")
    N = F * T
    WC = 3 * DF + FFF
    CH = D // C

    centered = x - jnp.mean(x, axis=1, keepdims=True)
    inv_scale = lax.rsqrt(jnp.mean(centered * centered, axis=1, keepdims=True) + norm_eps)
    xhat = centered * inv_scale

    q_rows = lax.dynamic_slice_in_dim(qkv_weight, c_index * R, R, 0)
    f_rows = lax.dynamic_slice_in_dim(fc1_weight, c_index * R, R, 0)
    w_send = jnp.concatenate(
        [
            q_rows.reshape(R, 3, F, DF).transpose(2, 0, 1, 3).reshape(F, R, 3 * DF),
            f_rows.reshape(R, F, FFF).transpose(1, 0, 2),
        ],
        axis=2,
    )
    small = jnp.concatenate(
        [ln1_gain, ln1_bias, ln2_gain, ln2_bias, out_bias, fc2_bias, qkv_bias]
    ).astype(F32)
    small_rows = -(-small.shape[0] // 1024) * 8
    small_in = jnp.pad(small, (0, small_rows * 128 - small.shape[0])).reshape(small_rows, 128)
    got = comm(
        1,
        F,
        C,
        {"w": w_send, "small": small_in, "xh": xhat.astype(BF), "gh": cot.astype(BF)},
        {
            "xa": ((F, T, D), BF),
            "ga": ((F, T, D), BF),
            "sa": ((F, small_rows, 128), F32),
            "wf": ((F, PN, 2, R, WC), BF),
        },
        {"wt": ((F, R, WC), BF)},
        [
            op_all_to_all("fsdp", "w", "wt"),
            op_gather("fsdp", "small", "sa"),
            op_gather("fsdp", "xh", "xa"),
            op_gather("fsdp", "gh", "ga"),
            (
                "plane",
                lambda r, g, p: r["wt"],
                lambda r, g: r["wf"].at[:, g.me, lax.rem(g.c, 2)],
                True,
                (0,),
            ),
            (
                "core",
                lambda r, g, p: r["wf"].at[:, :, g.me],
                lambda r, g: r["wf"].at[:, :, g.me],
                False,
                (4,),
            ),
        ],
    )
    w_all = got["wf"].reshape(D, WC)
    w_qkv = w_all[:, : 3 * DF]
    w_fc1 = w_all[:, 3 * DF :]
    small_all = got["sa"].reshape(F, small_rows * 128)
    vec = [small_all[:, i * DF : (i + 1) * DF].reshape(D) for i in range(6)]
    gain1, bias1, gain2, bias2, b_out, b_fc2 = vec
    b_qkv = small_all[:, 6 * DF : 9 * DF].reshape(3, F, DF)
    b_qkv = lax.dynamic_slice_in_dim(b_qkv, f_index, 1, 1).reshape(3 * DF)
    xh = got["xa"].reshape(N, D).astype(F32)
    gh = got["ga"].reshape(N, D)
    hidden1 = (xh * gain1 + bias1).astype(BF)
    hidden2 = (xh * gain2 + bias2).astype(BF)

    proj = dot(hidden1, w_qkv) + b_qkv
    positions = c_index * T + jnp.arange(T, dtype=jnp.int32)
    tables = rotary_tables(positions, 2 * DF)
    cos_t, sa_t, sb_t = (jnp.tile(t, (F, 1)) for t in tables)
    qk = proj[:, : 2 * DF]
    half = ROT // 2
    qk = qk * cos_t + jnp.roll(qk, -half, 1) * sa_t + jnp.roll(qk, half, 1) * sb_t
    grad_mixed = dot_nt(gh, out_weight).astype(BF)
    stack = jnp.concatenate(
        [qk.astype(BF), proj[:, 2 * DF :].astype(BF), grad_mixed], axis=1
    )
    pairs = DF // CH
    stack = stack.reshape(F, T, 4, pairs, CH).transpose(0, 3, 2, 1, 4).reshape(C, 4, T, CH)
    spread = comm(
        2,
        F,
        C,
        {"s": stack},
        {"d": ((4, C, T, CH), BF)},
        {},
        [("ctx", lambda r, g, p: r["s"].at[p], lambda r, g: r["d"].at[:, g.me], True, ())],
    )["d"]
    length_tables = rotary_tables(jnp.arange(C * T, dtype=jnp.int32), CH)
    heads = attention(spread.reshape(4, C * T, CH), length_tables)
    back = comm(
        3,
        F,
        C,
        {"s": heads.reshape(4, C, T, CH)},
        {"d": ((4, C, T, CH), BF)},
        {},
        [("ctx", lambda r, g, p: r["s"].at[:, p], lambda r, g: r["d"].at[:, g.me], True, ())],
    )["d"]
    back = back.reshape(4, F, pairs, T, CH).transpose(1, 3, 0, 2, 4).reshape(N, 4 * DF)
    mixed = back[:, :DF]
    grad_proj = back[:, DF:]

    pre_act = dot(hidden2, w_fc1) + fc1_bias.astype(F32)
    cdf = 0.5 * (1.0 + lax.erf(pre_act * root_half))
    activation = (pre_act * cdf).astype(BF)
    slope = cdf + pre_act * jnp.exp(-0.5 * pre_act * pre_act) * root_two_pi
    grad_pre = dot_nt(gh, fc2_weight) * slope
    grad_pre_half = grad_pre.astype(BF)
    grad_hidden2 = dot_nt(grad_pre_half, w_fc1)
    grad_hidden1 = dot_nt(grad_proj, w_qkv)

    y_part = dot(activation, fc2_weight) + dot(mixed, out_weight)
    g_part = grad_hidden1 * gain1 + grad_hidden2 * gain2
    yg = jnp.stack(
        [y_part.astype(BF).reshape(F, T, D), g_part.astype(BF).reshape(F, T, D)], axis=1
    )

    g_fc1 = dot_tn(hidden2, grad_pre_half).astype(BF).reshape(F, PN, 2, R, FFF)
    g_qkv = dot_tn(hidden1, grad_proj).astype(BF).reshape(F, PN, 2, R, 3 * DF)
    g_fc2 = dot_tn(activation, gh).astype(BF).reshape(PN, 2, RF, D)
    g_out = dot_tn(mixed, gh).astype(BF).reshape(PN, 2, R, D)
    cot_sum = jnp.sum(cot, axis=0)
    qkv_sum = jnp.sum(grad_proj.astype(F32), axis=0).reshape(3, 1, DF)
    mine = jnp.arange(F)[None, :, None] == f_index
    fc1_sum = jnp.sum(grad_pre, axis=0)
    mine_fc1 = jnp.arange(F)[:, None] == f_index
    vec_sums = jnp.concatenate(
        [
            jnp.sum(grad_hidden1 * xh, axis=0),
            jnp.sum(grad_hidden1, axis=0),
            jnp.sum(grad_hidden2 * xh, axis=0),
            jnp.sum(grad_hidden2, axis=0),
            cot_sum,
            jnp.where(mine, qkv_sum, 0.0).reshape(3 * D),
            jnp.where(mine_fc1, fc1_sum[None], 0.0).reshape(FF),
        ]
    )
    vec_total = lax.psum(vec_sums, ("ctx", "fsdp"))

    def other_core(name, wide):
        if wide:
            src = lambda r, g, p: r[name].at[:, :, p]
        else:
            src = lambda r, g, p: r[name].at[:, p]
        return ("core", src, lambda r, g: r[name + "_o"], False, ())

    got = comm(
        4,
        F,
        C,
        {"yg": yg, "fc1": g_fc1, "qkv": g_qkv, "fc2": g_fc2, "out": g_out},
        {
            "yga": ((F, 2, T, D), BF),
            "fc1_o": ((F, PN, R, FFF), BF),
            "qkv_o": ((F, PN, R, 3 * DF), BF),
            "fc2_o": ((PN, RF, D), BF),
            "out_o": ((PN, R, D), BF),
        },
        {},
        [
            op_all_to_all("fsdp", "yg", "yga"),
            other_core("fc1", True),
            other_core("qkv", True),
            other_core("fc2", False),
            other_core("out", False),
        ],
    )
    yg_sum = jnp.sum(got["yga"].astype(F32), axis=0)
    layer_rows = x + yg_sum[0] + (b_out + b_fc2)
    g = yg_sum[1]
    in_rows = cot + inv_scale * (
        g
        - jnp.mean(g, axis=1, keepdims=True)
        - xhat * jnp.mean(g * xhat, axis=1, keepdims=True)
    )

    core = lax.rem(c_index, 2)

    def own_core(array, axis):
        part = lax.dynamic_slice_in_dim(array, core, 1, axis)
        return lax.squeeze(part, (axis,))

    def add(a, b):
        return (a.astype(F32) + b.astype(F32)).astype(BF)

    h_fc1 = add(own_core(g_fc1, 2), got["fc1_o"]).transpose(1, 0, 2, 3)
    h_qkv = add(own_core(g_qkv, 2), got["qkv_o"]).transpose(1, 0, 2, 3)
    h_fc2 = add(own_core(g_fc2, 1), got["fc2_o"])
    h_out = add(own_core(g_out, 1), got["out_o"])
    halves = {"fc1": h_fc1, "qkv": h_qkv, "fc2": h_fc2, "out": h_out}
    got = comm(
        5,
        F,
        C,
        halves,
        {n + "_o": (a.shape, BF) for n, a in halves.items()},
        {},
        [op_all_to_all("plane", n, n + "_o") for n in halves],
    )
    red = {n: jnp.sum(got[n + "_o"].astype(F32), axis=0).astype(BF) for n in halves}

    def spread_core(name, number):
        view = lambda r, g: r[name].at[:, g.me]
        return ("core", lambda r, g, p: view(r, g), view, False, (number,))

    def spread_plane(src, name, after):
        return (
            "plane",
            lambda r, g, p: r[src],
            lambda r, g: r[name].at[g.me, lax.rem(g.c, 2)],
            True,
            after,
        )

    got = comm(
        6,
        F,
        C,
        red,
        {
            "fc1_o": ((PN, 2, F, R, FFF), BF),
            "qkv_o": ((PN, 2, F, R, 3 * DF), BF),
            "fc2_o": ((PN, 2, RF, D), BF),
            "out_o": ((PN, 2, R, D), BF),
        },
        {"fc1_t": ((F, R, FFF), BF), "qkv_t": ((F, R, 3 * DF), BF)},
        [
            op_all_to_all("fsdp", "fc1", "fc1_t"),
            op_all_to_all("fsdp", "qkv", "qkv_t"),
            spread_plane("fc2", "fc2_o", ()),
            spread_plane("out", "out_o", ()),
            spread_plane("fc1_t", "fc1_o", (0,)),
            spread_plane("qkv_t", "qkv_o", (1,)),
            spread_core("fc2_o", 2),
            spread_core("out_o", 3),
            spread_core("fc1_o", 4),
            spread_core("qkv_o", 5),
        ],
    )
    d_fc1 = (
        got["fc1_o"].reshape(C, F, R, FFF).transpose(0, 2, 1, 3).reshape(DF, FF).astype(F32)
    )
    d_qkv = (
        got["qkv_o"]
        .reshape(C, F, R, 3, DF)
        .transpose(0, 2, 3, 1, 4)
        .reshape(DF, 3 * D)
        .astype(F32)
    )
    d_fc2 = got["fc2_o"].reshape(FFF, D).astype(F32)
    d_out = got["out_o"].reshape(DF, D).astype(F32)

    def own_part(start, size):
        return lax.dynamic_slice_in_dim(
            vec_total[start : start + size], f_index * (size // F), size // F, 0
        )

    cot_total = own_part(4 * D, D)
    return (
        layer_rows[None],
        in_rows[None],
        own_part(0, D),
        own_part(D, D),
        own_part(2 * D, D),
        own_part(3 * D, D),
        d_qkv,
        own_part(5 * D, 3 * D),
        d_out,
        cot_total,
        d_fc1,
        own_part(8 * D, FF),
        d_fc2,
        cot_total,
    )


def solution(mesh):
    F, C = mesh.shape["fsdp"], mesh.shape["ctx"]
    rows, row, mat = P("fsdp", "ctx", None), P("fsdp"), P("fsdp", None)
    return jax.shard_map(
        functools.partial(on_device, F, C),
        mesh=mesh,
        in_specs=(rows, row, row, row, row, mat, row, mat, row, mat, row, mat, row, rows),
        out_specs=(rows, rows, row, row, row, row, mat, row, mat, row, mat, row, mat, row),
        check_vma=False,
    )
```

time: 1120 us -> 417 us (0.37)
  waiting for transfers between devices: 799 us -> 0 us
  Pallas kernels: 0 us -> 237 us
  blocking collectives: 125 us -> 50 us
  starting transfers between devices: 45.8 us -> 0 us
  matrix products: 58 us -> 24.1 us
  local copies, waits for them, and re-layouts: 30.6 us -> 61.6 us
  between operations: 16.4 us -> 1.6 us
    reduce_scatter x4 -> x0, waiting for transfers between devices: 410 us -> none  [the longest x1 148 us: on_device(): lax.psum_scatter(partials[8].astype(jnp.bfloat16), 'fsdp', scatter_dimens...]
    all_gather x6 -> x0, waiting for transfers between devices: 247 us -> none  [the longest x1 88.3 us: on_device(): lax.all_gather(fc2_weight, 'fsdp', axis=0, tiled=True)]
    pallas_call x0 -> x7, Pallas kernels: none -> 237 us  [the longest x6 227 us: comm(): pl.pallas_call(kernel, name='comm%d' % cid, out_shape=[jax.ShapeDtypeStru...]
    all_gather x8 -> x0, blocking collectives: 93.4 us -> none  [the longest x1 15 us: on_device(): lax.all_gather(feedforward_norm_bias, 'fsdp', axis=0, tiled=True)]
    ppermute x32 -> x0, waiting for transfers between devices: 88.3 us -> none  [from_behind(): lax.ppermute(array, axis, [(i, (i + by) % devices) for i in range(devices)])]
    psum x1 -> x0, waiting for transfers between devices: 52.3 us -> none  [on_device(): lax.psum(owned[4].astype(jnp.bfloat16), 'ctx').astype(jnp.float32)]
    ppermute x32 -> x0, starting transfers between devices: 45.4 us -> none  [from_behind(): lax.ppermute(array, axis, [(i, (i + by) % devices) for i in range(devices)])]
    psum x1, blocking collectives: 12.4 us -> 50 us  [on_device(): vec_total = lax.psum(vec_sums, ('ctx', 'fsdp'))]
  transfers between devices with their start and end apart: 43 -> 0, of which waited for: 42 -> 0; matrix products, arithmetic and copies ran while one was open for 9% -> 0% of each run, Pallas kernels for 0% -> 0%
where the time goes in v1:
time: 417 us; the launch traced here: 410 us
  Pallas kernels  237 us (57%)
  local copies, waits for them, and re-layouts  61.6 us (15%)
  blocking collectives  50 us (12%)
  other arithmetic  35.7 us (9%)
  matrix products  24.1 us (6%)
    pallas_call x6, Pallas kernels, comm(): pl.pallas_call(kernel, name='comm%d' % cid, out_shape=[jax.ShapeDtypeStru...  227 us
    psum x1, blocking collectives, on_device(): vec_total = lax.psum(vec_sums, ('ctx', 'fsdp'))  50 us
    convert_element_type x3, local copies, waits for them, and re-layouts, on_device(): d_qkv = got['qkv_o'].reshape(C, F, R, 3, DF).transpose(0, 2, 3, 1, 4).res...  16.9 us
    pallas_call x1, Pallas kernels, attention(): pl.pallas_call(attention_kernel, name='attention', out_shape=jax.ShapeDty...  9.82 us
    dot_general x4, matrix products, dot_nt(): lax.dot_general(a, b, (((1,), (1,)), ((), ())), preferred_element_type=F32)  9.32 us
    unnamed x91, local copies, waits for them, and re-layouts  9.03 us
    dot_general x4, matrix products, dot_tn(): lax.dot_general(a, b, (((0,), (0,)), ((), ())), preferred_element_type=F32)  8.7 us

profile of v1, /device:TPU:0, one launch (start us, length us, event | category | flops | bytes accessed | tf_op | source)
XLA Modules:
  0.0 410.1 jit_solution(13032965117296711182)
XLA Ops:
  0.8 1.1 constant_dynamic-slice_fusion.2
  1.9 1.6 constant_dynamic-slice_fusion.3
  3.5 1.8 reshape.269
  5.3 1.7 copy.56
  7.1 1.8 reshape.270
  8.9 1.7 pad_maximum_fusion.2.args_0_
  13.1 0.8 fusion.34.args_2_
  13.9 0.7 fusion.44
  14.7 62.3 %comm1.1 = (bf16[4,128,1024]{2,1,0:T(8,128)(2,1)}, bf16[4,128,1024]{2,1,0:T(8,128)(2,1)}, f32[4,24,128]{2,1,0:T(8,128)}, bf16[4,4,2,32,1792]{4,3,2,1,0:T(8,128)(2,1)}) custom-call(bf16[4,32,1792]{2,1,0:T(8,128)(2,1)} %pad_maximum_fusion.2.args_0_, f32[24,128]{1,0:T(8,128)} %bitcast_convert_fusion.2.args_1_, bf16[128,1024]{1,0:T(8,128)(2,1)} %fusion.34.args_2_, ...), custom_call_target="tpu_custom_call" | custom-call | tf_op jit(solution)/shard_map/comm1/pallas_call | solution.py:120
  76.9 0.9 copy.104
  77.9 2.4 convolution_convert_fusion.4
  80.3 1.9 fusion.8
  82.3 2.7 convolution_add_fusion
  85.0 0.8 slice.178
  85.8 0.9 fusion.42
  86.7 1.7 fusion.43
  89.1 0.7 tile.36
  89.9 1.1 copy.58
  91.0 2.6 fusion.24
  93.6 1.1 pad_maximum_fusion.1
  94.7 2.6 reshape.278
  97.3 2.4 copy.62
  99.7 15.1 %comm2.1 = bf16[4,8,128,128]{3,2,1,0:T(8,128)(2,1)} custom-call(bf16[8,4,128,128]{3,2,1,0:T(8,128)(2,1)} %bitcast.154), custom_call_target="tpu_custom_call" | custom-call | tf_op jit(solution)/shard_map/comm2/pallas_call | solution.py:120
  115.1 0.8 maximum_maximum_fusion.2
  115.9 1.0 copy.63.cos_ref
  116.9 1.0 tile.89
  117.9 1.0 copy.64.sa_ref
  119.0 1.0 copy.65.sb_ref
  120.0 9.8 %attention.1 = bf16[4,1024,128]{2,1,0:T(8,128)(2,1)} custom-call(bf16[4,1024,128]{2,1,0:T(8,128)(2,1)} %bitcast.151, f32[1024,128]{1,0:T(8,128)} %copy.63.cos_ref, f32[1024,128]{1,0:T(8,128)} %copy.64.sa_ref, f32[1024,128]{1,0:T(8,128)} %copy.65.sb_ref), custom_call_target="tpu_custom_call" | custom-call | tf_op jit(solution)/shard_map/attention/pallas_call | solution.py:198
  129.8 16.9 %comm3.1 = bf16[4,8,128,128]{3,2,1,0:T(8,128)(2,1)} custom-call(bf16[4,8,128,128]{3,2,1,0:T(8,128)(2,1)} %bitcast.152), custom_call_target="tpu_custom_call" | custom-call | tf_op jit(solution)/shard_map/comm3/pallas_call | solution.py:120
  146.7 3.3 copy.102
  150.0 2.6 reshape.283
  152.6 2.8 fusion.18
  155.6 1.7 multiply_convert_fusion
  157.3 2.4 fusion.46
  159.7 1.7 fusion.40
  161.5 1.3 fusion.47
  163.3 1.5 pad_maximum_fusion.args_0_
  164.8 2.6 convolution_convert_fusion.1
  167.4 2.2 convolution_convert_fusion.2
  169.6 2.6 convolution_convert_fusion
  172.2 1.3 convolution_convert_fusion.3
  173.5 49.2 %comm4.1 = (bf16[4,2,128,1024]{3,2,1,0:T(8,128)(2,1)}, bf16[4,4,32,1024]{3,2,1,0:T(8,128)(2,1)}, bf16[4,4,32,768]{3,2,1,0:T(8,128)(2,1)}, bf16[4,128,1024]{2,1,0:T(8,128)(2,1)}, bf16[4,32,1024]{2,1,0:T(8,128)(2,1)}) custom-call(bf16[4,2,128,1024]{3,2,1,0:T(8,128)(2,1)} %pad_maximum_fusion.args_0_, bf16[4,4,2,32,1024]{4,3,2,1,0:T(8,128)(2,1)} %bitcast.149, ...), custom_call_target="tpu_custom_call" | custom-call | tf_op jit(solution)/shard_map/comm4/pallas_call | solution.py:120
  222.8 2.1 convert_reduce_fusion
  225.3 1.1 multiply_add_fusion
  226.7 50.0 %psum.7 = f32[12288]{0:T(1024)S(1)} all-reduce(f32[12288]{0:T(1024)S(1)} %bitcast_dynamic-update-slice_fusion), channel_id=1, replica_groups=mesh['ctx'=8,'fsdp'=4] {'ctx','fsdp'}, use_global_device_ids=true, to_apply=%region_12.13 | all-reduce | flops 12288 | bytes 98304 | tf_op jit(solution)/shard_map/psum | solution.py:403
  279.3 3.1 fusion.21.args_0_
  282.4 2.2 fusion.25.args_1_
  284.6 1.4 fusion.11.args_2_
  286.0 0.8 fusion.29.args_3_
  286.8 40.0 %comm5.1 = (bf16[4,4,32,1024]{3,2,1,0:T(8,128)(2,1)}, bf16[4,4,32,768]{3,2,1,0:T(8,128)(2,1)}, bf16[4,128,1024]{2,1,0:T(8,128)(2,1)}, bf16[4,32,1024]{2,1,0:T(8,128)(2,1)}) custom-call(bf16[4,4,32,1024]{3,2,1,0:T(8,128)(2,1)} %fusion.21.args_0_, bf16[4,4,32,768]{3,2,1,0:T(8,128)(2,1)} %fusion.25.args_1_, bf16[4,128,1024]{2,1,0:T(8,128)(2,1)} %fusion.11.args_2_, ...), custom_call_target="tpu_custom_call" | custom-call | tf_op jit(solution)/shard_map/comm5/pallas_call | solution.py:120
  326.8 2.3 reduce_sum.168.args_0_
  329.1 2.0 reduce_sum.169.args_1_
  331.1 0.9 reduce_sum.170.args_2_
  332.0 0.7 reduce_sum.171.args_3_
  332.7 43.8 %comm6.1 = (bf16[4,2,4,32,1024]{4,3,2,1,0:T(8,128)(2,1)}, bf16[4,2,4,32,768]{4,3,2,1,0:T(8,128)(2,1)}, bf16[4,2,128,1024]{3,2,1,0:T(8,128)(2,1)}, bf16[4,2,32,1024]{3,2,1,0:T(8,128)(2,1)}) custom-call(bf16[4,32,1024]{2,1,0:T(8,128)(2,1)} %reduce_sum.168.args_0_, bf16[4,32,768]{2,1,0:T(8,128)(2,1)} %reduce_sum.169.args_1_, ...), custom_call_target="tpu_custom_call" | custom-call | tf_op jit(solution)/shard_map/comm6/pallas_call | solution.py:120
  376.5 5.6 %reshape.299 = f32[8,4,32,3,256]{4,3,2,1,0:T(4,128)} reshape(bf16[4,2,4,32,768]{4,3,2,1,0:T(8,128)(2,1)} %get-tuple-element.44) | data formatting | bytes 4718592 | tf_op jit(solution)/shard_map/convert_element_type | solution.py:513
  382.1 5.9 %copy.73 = f32[8,32,3,4,256]{4,3,2,1,0:T(4,128)} copy(f32[8,32,3,4,256]{4,2,1,3,0:T(4,128)} %bitcast.145) | data formatting | bytes 6291456 | tf_op jit(solution)/shard_map/convert_element_type | solution.py:513
  388.0 5.5 %reshape.295 = f32[256,3072]{1,0:T(8,128)} reshape(f32[8,32,3,4,256]{4,3,2,1,0:T(4,128)} %copy.73) | data formatting | bytes 6291456 | tf_op jit(solution)/shard_map/convert_element_type | solution.py:513
  393.5 0.7 dynamic_slice.53
  394.1 1.1 bitcast_convert_fusion.1
  395.9 2.7 copy.74
  398.7 5.8 %copy.89 = f32[32,8,4,1024]{3,1,2,0:T(8,128)} copy(f32[32,8,4,1024]{3,2,1,0:T(4,128)S(1)} %bitcast.146) | data formatting | bytes 8388608
  405.1 4.2 %bitcast_convert_fusion = f32[1024,1024]{1,0:T(8,128)} fusion(bf16[4,2,128,1024]{3,2,1,0:T(8,128)(2,1)} %get-tuple-element.47), kind=kLoop, calls=%fused_computation.19 | loop fusion | flops 1048576 | bytes 6291456 | tf_op jit(solution)/shard_map/convert_element_type | solution.py:515
  (142 shorter events, 9.4 us)
Async XLA Ops:
  0.6 156.7 %copy-start = (bf16[1024,1024]{1,0:T(8,128)(2,1)S(1)}, bf16[1024,1024]{1,0:T(8,128)(2,1)}, u32[]{:S(2)}) copy-start(bf16[1024,1024]{1,0:T(8,128)(2,1)} %param.25) | copy-start | bytes 6291460
  0.7 12.1 %copy-start.2 = (f32[1,128,1024]{2,1,0:T(8,128)S(1)}, f32[1,128,1024]{2,1,0:T(8,128)}, u32[]{:S(2)}) copy-start(f32[1,128,1024]{2,1,0:T(8,128)} %param.14) | copy-start | bytes 1572868
  0.7 10.0 %copy-start.28 = (bf16[256]{0:T(256)(128)(2,1)S(1)}, bf16[256]{0:T(256)(128)(2,1)}, u32[]{:S(2)}) copy-start(bf16[256]{0:T(256)(128)(2,1)} %param.15) | copy-start | bytes 1540
  0.7 10.1 %copy-start.29 = (bf16[256]{0:T(256)(128)(2,1)S(1)}, bf16[256]{0:T(256)(128)(2,1)}, u32[]{:S(2)}) copy-start(bf16[256]{0:T(256)(128)(2,1)} %param.16) | copy-start | bytes 1540
  0.7 10.3 %copy-start.30 = (bf16[256]{0:T(256)(128)(2,1)S(1)}, bf16[256]{0:T(256)(128)(2,1)}, u32[]{:S(2)}) copy-start(bf16[256]{0:T(256)(128)(2,1)} %param.17) | copy-start | bytes 1540
  0.7 10.5 %copy-start.31 = (bf16[256]{0:T(256)(128)(2,1)S(1)}, bf16[256]{0:T(256)(128)(2,1)}, u32[]{:S(2)}) copy-start(bf16[256]{0:T(256)(128)(2,1)} %param.18) | copy-start | bytes 1540
  0.7 10.8 %copy-start.32 = (bf16[256]{0:T(256)(128)(2,1)S(1)}, bf16[256]{0:T(256)(128)(2,1)}, u32[]{:S(2)}) copy-start(bf16[256]{0:T(256)(128)(2,1)} %param.22) | copy-start | bytes 1540
  0.7 11.0 %copy-start.33 = (bf16[256]{0:T(256)(128)(2,1)S(1)}, bf16[256]{0:T(256)(128)(2,1)}, u32[]{:S(2)}) copy-start(bf16[256]{0:T(256)(128)(2,1)} %param.26) | copy-start | bytes 1540
  0.7 11.2 %copy-start.27 = (bf16[768]{0:T(1024)(128)(2,1)S(1)}, bf16[768]{0:T(1024)(128)(2,1)}, u32[]{:S(2)}) copy-start(bf16[768]{0:T(1024)(128)(2,1)} %param.20) | copy-start | bytes 4612
  3.5 10.4 %copy-start.8 = (f32[1,128,1024]{2,1,0:T(8,128)S(1)}, f32[1,128,1024]{2,1,0:T(8,128)}, u32[]{:S(2)}) copy-start(f32[1,128,1024]{2,1,0:T(8,128)} %param.27) | copy-start | bytes 1572868
  12.8 65.0 %copy-start.19 = (bf16[256,1024]{1,0:T(8,128)(2,1)S(1)}, bf16[256,1024]{1,0:T(8,128)(2,1)}, u32[]{:S(2)}) copy-start(bf16[256,1024]{1,0:T(8,128)(2,1)} %param.21) | copy-start | bytes 1572868
  76.9 3.4 copy-start.10
  85.0 3.4 copy-start.3
  91.0 2.6 copy-start.17
  91.0 2.6 copy-start.24
  152.6 2.8 copy-start.26
  152.6 2.8 copy-start.13
  152.6 3.1 copy-start.34
  155.6 1.7 copy-start.14
  157.3 2.4 copy-start.11
  161.5 1.3 copy-start.4
  161.5 1.3 copy-start.20
  164.8 2.6 copy-start.12
  222.7 2.5 copy-start.9
  226.5 55.8 %copy-start.18 = (bf16[4,4,32,768]{3,2,1,0:T(8,128)(2,1)S(1)}, bf16[4,4,32,768]{3,2,1,0:T(8,128)(2,1)}, u32[]{:S(2)}) copy-start(bf16[4,4,32,768]{3,2,1,0:T(8,128)(2,1)} %get-tuple-element.37) | copy-start | bytes 2359300
  279.3 5.3 %copy-start.5 = (bf16[1024,1024]{1,0:T(8,128)(2,1)S(1)}, bf16[1024,1024]{1,0:T(8,128)(2,1)}, u32[]{:S(2)}) copy-start(bf16[1024,1024]{1,0:T(8,128)(2,1)} %convolution_convert_fusion) | copy-start | bytes 6291460
  279.3 5.3 %copy-start.16 = (bf16[4,128,1024]{2,1,0:T(8,128)(2,1)S(1)}, bf16[4,128,1024]{2,1,0:T(8,128)(2,1)}, u32[]{:S(2)}) copy-start(bf16[4,128,1024]{2,1,0:T(8,128)(2,1)} %get-tuple-element.38) | copy-start | bytes 3145732
  284.6 1.4 copy-start.6
  284.6 1.4 copy-start.23
  326.8 4.3 %copy-start.15 = (bf16[4,128,1024]{2,1,0:T(8,128)(2,1)S(1)}, bf16[4,128,1024]{2,1,0:T(8,128)(2,1)}, u32[]{:S(2)}) copy-start(bf16[4,128,1024]{2,1,0:T(8,128)(2,1)} %get-tuple-element.42) | copy-start | bytes 3145732
  326.8 5.2 %copy-start.22 = (bf16[4,32,1024]{2,1,0:T(8,128)(2,1)S(1)}, bf16[4,32,1024]{2,1,0:T(8,128)(2,1)}, u32[]{:S(2)}) copy-start(bf16[4,32,1024]{2,1,0:T(8,128)(2,1)} %get-tuple-element.43) | copy-start | bytes 786436
  387.9 6.2 %copy-start.21 = (bf16[4,2,32,1024]{3,2,1,0:T(8,128)(2,1)S(1)}, bf16[4,2,32,1024]{3,2,1,0:T(8,128)(2,1)}, u32[]{:S(2)}) copy-start(bf16[4,2,32,1024]{3,2,1,0:T(8,128)(2,1)} %get-tuple-element.45) | copy-start | bytes 1572868
  387.9 7.4 %copy-start.7 = (bf16[4,2,4,32,1024]{4,3,2,1,0:T(8,128)(2,1)S(1)}, bf16[4,2,4,32,1024]{4,3,2,1,0:T(8,128)(2,1)}, u32[]{:S(2)}) copy-start(bf16[4,2,4,32,1024]{4,3,2,1,0:T(8,128)(2,1)} %get-tuple-element.46) | copy-start | bytes 6291460
  395.3 14.0 %copy-start.25 = (f32[256]{0:T(256)}, f32[256]{0:T(256)S(1)}, u32[]{:S(2)}) copy-start(f32[256]{0:T(256)S(1)} %dynamic_slice.54) | copy-start | bytes 3076
  405.1 4.8 %copy-start.1 = (bf16[1024,1024]{1,0:T(8,128)(2,1)S(1)}, bf16[1024,1024]{1,0:T(8,128)(2,1)}, u32[]{:S(2)}) copy-start(bf16[1024,1024]{1,0:T(8,128)(2,1)} %param.25) | copy-start | bytes 6291460

commit v2 on v1

--- a/solution.py
+++ b/solution.py
@@ -57,12 +57,14 @@
 }
 
 
-def comm(cid, F, C, inputs, outputs, scratch, ops):
+def comm(cid, F, C, inputs, outputs, scratch, ops, relays=()):
     names = list(inputs) + list(outputs) + list(scratch)
-    sizes = [GROUP_SIZE[op[0]](F, C) for op in ops]
+    sizes = [GROUP_SIZE[op[0]](F, C) if op[0] else 0 for op in ops]
     offset = [sum(sizes[:i]) for i in range(len(ops))]
-    total = sum(sizes)
-    used = sorted({op[0] for op in ops})
+    relay_at = sum(sizes)
+    steps = F - 1
+    total = relay_at + len(relays) * (2 * steps + 1)
+    used = sorted({op[0] for op in ops if op[0]})
 
     def kernel(*args):
         refs = dict(zip(names, args))
@@ -83,6 +85,68 @@
         started = {}
         done = set()
 
+        def relay_copy(i, way, t, index):
+            src, dst = relays[i]
+            slot = relay_at + (2 * i + (way > 0)) * steps + t
+            f = groups["fsdp"].f
+            return pltpu.make_async_remote_copy(
+                src_ref=refs[src] if t == 0 else refs[dst].at[index],
+                dst_ref=refs[dst].at[index],
+                send_sem=send_sem.at[slot],
+                recv_sem=recv_sem.at[slot],
+                device_id={"fsdp": lax.rem(f + way + F, F)},
+                device_id_type=MESH,
+            )
+
+        def relay_sends(way, t):
+            f = groups["fsdp"].f
+            source, target = f - way * t, f + way
+            return source, (source >= 0) & (source < F) & (target >= 0) & (target < F)
+
+        def relay_start(t):
+            for i in range(len(relays)):
+                for way in (1, -1):
+                    source, go = relay_sends(way, t)
+
+                    @pl.when(go)
+                    def _():
+                        relay_copy(i, way, t, source).start()
+
+        def relay_receive(t):
+            for i in range(len(relays)):
+                for way in (1, -1):
+                    source = groups["fsdp"].f - way * (t + 1)
+
+                    @pl.when((source >= 0) & (source < F))
+                    def _():
+                        relay_copy(i, way, t, source).wait_recv()
+
+        def relay_own(i):
+            src, dst = relays[i]
+            return pltpu.make_async_copy(
+                refs[src], refs[dst].at[groups["fsdp"].f], send_sem.at[total - 1 - i]
+            )
+
+        def relay_begin():
+            relay_start(0)
+            for i in range(len(relays)):
+                relay_own(i).start()
+
+        def relay_rest():
+            for t in range(steps):
+                relay_receive(t)
+                if t + 1 < steps:
+                    relay_start(t + 1)
+            for i in range(len(relays)):
+                relay_own(i).wait()
+                for way in (1, -1):
+                    for t in range(steps):
+                        source, go = relay_sends(way, t)
+
+                        @pl.when(go)
+                        def _():
+                            relay_copy(i, way, t, source).wait_send()
+
         def finish(i):
             if i in done:
                 return
@@ -90,9 +154,20 @@
             for copy in started[i]:
                 copy.wait()
 
+        relay_state = 0
         for i, (gname, src_view, dst_view, own, after) in enumerate(ops):
+            if relays and after and relay_state == 0:
+                relay_begin()
+                relay_state = 1
             for j in after:
                 finish(j)
+            if relays and relay_state == 1 and any(ops[j][4] for j in after):
+                relay_rest()
+                relay_state = 2
+            if gname is None:
+                src_view(refs, groups)
+                started[i] = []
+                continue
             g = groups[gname]
             copies = []
             for k in range(1, g.n):
@@ -114,6 +189,10 @@
                 copy.start()
                 copies.append(copy)
             started[i] = copies
+        if relays and relay_state == 0:
+            relay_begin()
+        if relays and relay_state < 2:
+            relay_rest()
         for i in range(len(ops)):
             finish(i)
 
@@ -268,15 +347,17 @@
     inv_scale = lax.rsqrt(jnp.mean(centered * centered, axis=1, keepdims=True) + norm_eps)
     xhat = centered * inv_scale
 
-    q_rows = lax.dynamic_slice_in_dim(qkv_weight, c_index * R, R, 0)
-    f_rows = lax.dynamic_slice_in_dim(fc1_weight, c_index * R, R, 0)
-    w_send = jnp.concatenate(
-        [
-            q_rows.reshape(R, 3, F, DF).transpose(2, 0, 1, 3).reshape(F, R, 3 * DF),
-            f_rows.reshape(R, F, FFF).transpose(1, 0, 2),
-        ],
-        axis=2,
-    )
+    def send_columns(name, stride, width, j, at):
+        return (
+            "fsdp",
+            lambda r, g, p: r[name].at[
+                g.c, :, pl.ds(pl.multiple_of(j * stride + p * width, 128), width)
+            ],
+            lambda r, g: r["wt"].at[g.me, :, pl.ds(at, width)],
+            True,
+            (),
+        )
+
     small = jnp.concatenate(
         [ln1_gain, ln1_bias, ln2_gain, ln2_bias, out_bias, fc2_bias, qkv_bias]
     ).astype(F32)
@@ -286,7 +367,13 @@
         1,
         F,
         C,
-        {"w": w_send, "small": small_in, "xh": xhat.astype(BF), "gh": cot.astype(BF)},
+        {
+            "qkv": qkv_weight.reshape(C, R, 3 * D),
+            "fc1": fc1_weight.reshape(C, R, FF),
+            "small": small_in,
+            "xh": xhat.astype(BF),
+            "gh": cot.astype(BF),
+        },
         {
             "xa": ((F, T, D), BF),
             "ga": ((F, T, D), BF),
@@ -295,25 +382,27 @@
         },
         {"wt": ((F, R, WC), BF)},
         [
-            op_all_to_all("fsdp", "w", "wt"),
+            send_columns("qkv", D, DF, 0, 0),
+            send_columns("qkv", D, DF, 1, DF),
+            send_columns("qkv", D, DF, 2, 2 * DF),
+            send_columns("fc1", 0, FFF, 0, 3 * DF),
             op_gather("fsdp", "small", "sa"),
-            op_gather("fsdp", "xh", "xa"),
-            op_gather("fsdp", "gh", "ga"),
             (
                 "plane",
                 lambda r, g, p: r["wt"],
                 lambda r, g: r["wf"].at[:, g.me, lax.rem(g.c, 2)],
                 True,
-                (0,),
+                (0, 1, 2, 3),
             ),
             (
                 "core",
                 lambda r, g, p: r["wf"].at[:, :, g.me],
                 lambda r, g: r["wf"].at[:, :, g.me],
                 False,
-                (4,),
+                (5,),
             ),
         ],
+        [("xh", "xa"), ("gh", "ga")],
     )
     w_all = got["wf"].reshape(D, WC)
     w_qkv = w_all[:, : 3 * DF]
@@ -328,6 +417,33 @@
     hidden1 = (xh * gain1 + bias1).astype(BF)
     hidden2 = (xh * gain2 + bias2).astype(BF)
 
+    pre_act = dot(hidden2, w_fc1) + fc1_bias.astype(F32)
+    cdf = 0.5 * (1.0 + lax.erf(pre_act * root_half))
+    activation = (pre_act * cdf).astype(BF)
+    slope = cdf + pre_act * jnp.exp(-0.5 * pre_act * pre_act) * root_two_pi
+    grad_pre = dot_nt(gh, fc2_weight) * slope
+    grad_pre_half = grad_pre.astype(BF)
+    grad_hidden2 = dot_nt(grad_pre_half, w_fc1)
+    g_fc1 = dot_tn(hidden2, grad_pre_half).astype(BF).reshape(F, PN, 2, R, FFF)
+    g_fc2 = dot_tn(activation, gh).astype(BF).reshape(PN, 2, RF, D)
+    y_ff = dot(activation, fc2_weight)
+
+    core = lax.rem(c_index, 2)
+
+    def own_core(array, axis):
+        part = lax.dynamic_slice_in_dim(array, core, 1, axis)
+        return lax.squeeze(part, (axis,))
+
+    def add(a, b):
+        return (a.astype(F32) + b.astype(F32)).astype(BF)
+
+    def other_core(name, wide):
+        if wide:
+            src = lambda r, g, p: r[name].at[:, :, p]
+        else:
+            src = lambda r, g, p: r[name].at[:, p]
+        return ("core", src, lambda r, g: r[name + "_o"], False, ())
+
     proj = dot(hidden1, w_qkv) + b_qkv
     positions = c_index * T + jnp.arange(T, dtype=jnp.int32)
     tables = rotary_tables(positions, 2 * DF)
@@ -341,15 +457,26 @@
     )
     pairs = DF // CH
     stack = stack.reshape(F, T, 4, pairs, CH).transpose(0, 3, 2, 1, 4).reshape(C, 4, T, CH)
-    spread = comm(
+    got = comm(
         2,
         F,
         C,
-        {"s": stack},
-        {"d": ((4, C, T, CH), BF)},
+        {"s": stack, "fc1": g_fc1, "fc2": g_fc2},
+        {
+            "d": ((4, C, T, CH), BF),
+            "fc1_o": ((F, PN, R, FFF), BF),
+            "fc2_o": ((PN, RF, D), BF),
+        },
         {},
-        [("ctx", lambda r, g, p: r["s"].at[p], lambda r, g: r["d"].at[:, g.me], True, ())],
-    )["d"]
+        [
+            ("ctx", lambda r, g, p: r["s"].at[p], lambda r, g: r["d"].at[:, g.me], True, ()),
+            other_core("fc1", True),
+            other_core("fc2", False),
+        ],
+    )
+    spread = got["d"]
+    h_fc1 = add(own_core(g_fc1, 2), got["fc1_o"]).transpose(1, 0, 2, 3)
+    h_fc2 = add(own_core(g_fc2, 1), got["fc2_o"])
     length_tables = rotary_tables(jnp.arange(C * T, dtype=jnp.int32), CH)
     heads = attention(spread.reshape(4, C * T, CH), length_tables)
     back = comm(
@@ -365,24 +492,15 @@
     mixed = back[:, :DF]
     grad_proj = back[:, DF:]
 
-    pre_act = dot(hidden2, w_fc1) + fc1_bias.astype(F32)
-    cdf = 0.5 * (1.0 + lax.erf(pre_act * root_half))
-    activation = (pre_act * cdf).astype(BF)
-    slope = cdf + pre_act * jnp.exp(-0.5 * pre_act * pre_act) * root_two_pi
-    grad_pre = dot_nt(gh, fc2_weight) * slope
-    grad_pre_half = grad_pre.astype(BF)
-    grad_hidden2 = dot_nt(grad_pre_half, w_fc1)
     grad_hidden1 = dot_nt(grad_proj, w_qkv)
 
-    y_part = dot(activation, fc2_weight) + dot(mixed, out_weight)
+    y_part = y_ff + dot(mixed, out_weight)
     g_part = grad_hidden1 * gain1 + grad_hidden2 * gain2
     yg = jnp.stack(
         [y_part.astype(BF).reshape(F, T, D), g_part.astype(BF).reshape(F, T, D)], axis=1
     )
 
-    g_fc1 = dot_tn(hidden2, grad_pre_half).astype(BF).reshape(F, PN, 2, R, FFF)
     g_qkv = dot_tn(hidden1, grad_proj).astype(BF).reshape(F, PN, 2, R, 3 * DF)
-    g_fc2 = dot_tn(activation, gh).astype(BF).reshape(PN, 2, RF, D)
     g_out = dot_tn(mixed, gh).astype(BF).reshape(PN, 2, R, D)
     cot_sum = jnp.sum(cot, axis=0)
     qkv_sum = jnp.sum(grad_proj.astype(F32), axis=0).reshape(3, 1, DF)
@@ -391,43 +509,71 @@
     mine_fc1 = jnp.arange(F)[:, None] == f_index
     vec_sums = jnp.concatenate(
         [
-            jnp.sum(grad_hidden1 * xh, axis=0),
-            jnp.sum(grad_hidden1, axis=0),
-            jnp.sum(grad_hidden2 * xh, axis=0),
-            jnp.sum(grad_hidden2, axis=0),
-            cot_sum,
-            jnp.where(mine, qkv_sum, 0.0).reshape(3 * D),
-            jnp.where(mine_fc1, fc1_sum[None], 0.0).reshape(FF),
-        ]
-    )
-    vec_total = lax.psum(vec_sums, ("ctx", "fsdp"))
-
-    def other_core(name, wide):
-        if wide:
+            jnp.sum(grad_hidden1 * xh, axis=0).reshape(F, DF),
+            jnp.sum(grad_hidden1, axis=0).reshape(F, DF),
+            jnp.sum(grad_hidden2 * xh, axis=0).reshape(F, DF),
+            jnp.sum(grad_hidden2, axis=0).reshape(F, DF),
+            cot_sum.reshape(F, DF),
+            jnp.where(mine, qkv_sum, 0.0).reshape(F, 3 * DF),
+            jnp.where(mine_fc1, fc1_sum[None], 0.0),
+        ],
+        axis=1,
+    )
+    VR = -(-vec_sums.shape[1] // 1024) * 8
+    vec_sums = jnp.pad(vec_sums, ((0, 0), (0, VR * 128 - vec_sums.shape[1])))
+
+    def sum_cores(r, groups):
+        own = groups["core"].me
+        for i in range(PN):
+            r["qkv_h"][i] = (
+                r["qkv"][:, i, own].astype(F32) + r["qkv_i"][:, i].astype(F32)
+            ).astype(BF)
+        for i in range(PN):
+            r["out_h"][i] = (r["out"][i, own].astype(F32) + r["out_i"][i].astype(F32)).astype(BF)
+
+    def into(name, dst):
+        if name == "qkv":
             src = lambda r, g, p: r[name].at[:, :, p]
         else:
             src = lambda r, g, p: r[name].at[:, p]
-        return ("core", src, lambda r, g: r[name + "_o"], False, ())
+        return ("core", src, lambda r, g: r[dst], False, ())
 
     got = comm(
         4,
         F,
         C,
-        {"yg": yg, "fc1": g_fc1, "qkv": g_qkv, "fc2": g_fc2, "out": g_out},
+        {
+            "yg": yg,
+            "vec": vec_sums.reshape(F, VR, 128),
+            "qkv": g_qkv,
+            "out": g_out,
+            "fc1_h": h_fc1,
+            "fc2_h": h_fc2,
+        },
         {
             "yga": ((F, 2, T, D), BF),
-            "fc1_o": ((F, PN, R, FFF), BF),
-            "qkv_o": ((F, PN, R, 3 * DF), BF),
+            "vec_o": ((F, VR, 128), F32),
+            "fc1_o": ((PN, F, R, FFF), BF),
             "fc2_o": ((PN, RF, D), BF),
+            "qkv_o": ((PN, F, R, 3 * DF), BF),
             "out_o": ((PN, R, D), BF),
         },
-        {},
+        {
+            "qkv_i": ((F, PN, R, 3 * DF), BF),
+            "out_i": ((PN, R, D), BF),
+            "qkv_h": ((PN, F, R, 3 * DF), BF),
+            "out_h": ((PN, R, D), BF),
+        },
         [
+            into("qkv", "qkv_i"),
+            into("out", "out_i"),
+            op_all_to_all("fsdp", "vec", "vec_o"),
             op_all_to_all("fsdp", "yg", "yga"),
-            other_core("fc1", True),
-            other_core("qkv", True),
-            other_core("fc2", False),
-            other_core("out", False),
+            op_all_to_all("plane", "fc1_h", "fc1_o"),
+            op_all_to_all("plane", "fc2_h", "fc2_o"),
+            (None, sum_cores, None, False, (0, 1)),
+            op_all_to_all("plane", "qkv_h", "qkv_o"),
+            op_all_to_all("plane", "out_h", "out_o"),
         ],
     )
     yg_sum = jnp.sum(got["yga"].astype(F32), axis=0)
@@ -439,30 +585,9 @@
         - xhat * jnp.mean(g * xhat, axis=1, keepdims=True)
     )
 
-    core = lax.rem(c_index, 2)
-
-    def own_core(array, axis):
-        part = lax.dynamic_slice_in_dim(array, core, 1, axis)
-        return lax.squeeze(part, (axis,))
-
-    def add(a, b):
-        return (a.astype(F32) + b.astype(F32)).astype(BF)
-
-    h_fc1 = add(own_core(g_fc1, 2), got["fc1_o"]).transpose(1, 0, 2, 3)
-    h_qkv = add(own_core(g_qkv, 2), got["qkv_o"]).transpose(1, 0, 2, 3)
-    h_fc2 = add(own_core(g_fc2, 1), got["fc2_o"])
-    h_out = add(own_core(g_out, 1), got["out_o"])
-    halves = {"fc1": h_fc1, "qkv": h_qkv, "fc2": h_fc2, "out": h_out}
-    got = comm(
-        5,
-        F,
-        C,
-        halves,
-        {n + "_o": (a.shape, BF) for n, a in halves.items()},
-        {},
-        [op_all_to_all("plane", n, n + "_o") for n in halves],
-    )
-    red = {n: jnp.sum(got[n + "_o"].astype(F32), axis=0).astype(BF) for n in halves}
+    names = ("fc1", "qkv", "fc2", "out")
+    vec_own = jnp.sum(got["vec_o"], axis=0)
+    red = {n: jnp.sum(got[n + "_o"].astype(F32), axis=0).astype(BF) for n in names}
 
     def spread_core(name, number):
         view = lambda r, g: r[name].at[:, g.me]
@@ -477,63 +602,69 @@
             after,
         )
 
+    def to_columns(name, dst, stride, width, j):
+        return (
+            "fsdp",
+            lambda r, g, p: r[name].at[p, :, pl.ds(j * width, width)],
+            lambda r, g: r[dst].at[
+                :, pl.ds(pl.multiple_of(j * stride + g.me * width, 128), width)
+            ],
+            True,
+            (),
+        )
+
     got = comm(
         6,
         F,
         C,
-        red,
+        {**red, "vec": vec_own},
         {
-            "fc1_o": ((PN, 2, F, R, FFF), BF),
-            "qkv_o": ((PN, 2, F, R, 3 * DF), BF),
+            "fc1_o": ((PN, 2, R, FF), BF),
+            "qkv_o": ((PN, 2, R, 3 * D), BF),
             "fc2_o": ((PN, 2, RF, D), BF),
             "out_o": ((PN, 2, R, D), BF),
+            "vec_o": ((C, VR, 128), F32),
         },
-        {"fc1_t": ((F, R, FFF), BF), "qkv_t": ((F, R, 3 * DF), BF)},
+        {"fc1_t": ((R, FF), BF), "qkv_t": ((R, 3 * D), BF)},
         [
-            op_all_to_all("fsdp", "fc1", "fc1_t"),
-            op_all_to_all("fsdp", "qkv", "qkv_t"),
+            op_gather("ctx", "vec", "vec_o"),
+            to_columns("fc1", "fc1_t", 0, FFF, 0),
+            to_columns("qkv", "qkv_t", D, DF, 0),
+            to_columns("qkv", "qkv_t", D, DF, 1),
+            to_columns("qkv", "qkv_t", D, DF, 2),
             spread_plane("fc2", "fc2_o", ()),
             spread_plane("out", "out_o", ()),
-            spread_plane("fc1_t", "fc1_o", (0,)),
-            spread_plane("qkv_t", "qkv_o", (1,)),
-            spread_core("fc2_o", 2),
-            spread_core("out_o", 3),
-            spread_core("fc1_o", 4),
-            spread_core("qkv_o", 5),
+            spread_plane("fc1_t", "fc1_o", (1,)),
+            spread_plane("qkv_t", "qkv_o", (2, 3, 4)),
+            spread_core("fc2_o", 5),
+            spread_core("out_o", 6),
+            spread_core("fc1_o", 7),
+            spread_core("qkv_o", 8),
         ],
     )
-    d_fc1 = (
-        got["fc1_o"].reshape(C, F, R, FFF).transpose(0, 2, 1, 3).reshape(DF, FF).astype(F32)
-    )
-    d_qkv = (
-        got["qkv_o"]
-        .reshape(C, F, R, 3, DF)
-        .transpose(0, 2, 3, 1, 4)
-        .reshape(DF, 3 * D)
-        .astype(F32)
-    )
+    d_fc1 = got["fc1_o"].reshape(DF, FF).astype(F32)
+    d_qkv = got["qkv_o"].reshape(DF, 3 * D).astype(F32)
     d_fc2 = got["fc2_o"].reshape(FFF, D).astype(F32)
     d_out = got["out_o"].reshape(DF, D).astype(F32)
+    vec_total = jnp.sum(got["vec_o"], axis=0).reshape(VR * 128)
 
     def own_part(start, size):
-        return lax.dynamic_slice_in_dim(
-            vec_total[start : start + size], f_index * (size // F), size // F, 0
-        )
-
-    cot_total = own_part(4 * D, D)
+        return vec_total[start * DF : start * DF + size]
+
+    cot_total = own_part(4, DF)
     return (
         layer_rows[None],
         in_rows[None],
-        own_part(0, D),
-        own_part(D, D),
-        own_part(2 * D, D),
-        own_part(3 * D, D),
+        own_part(0, DF),
+        own_part(1, DF),
+        own_part(2, DF),
+        own_part(3, DF),
         d_qkv,
-        own_part(5 * D, 3 * D),
+        own_part(5, 3 * DF),
         d_out,
         cot_total,
         d_fc1,
-        own_part(8 * D, FF),
+        own_part(8, FFF),
         d_fc2,
         cot_total,
     )

time: 417 us -> 311 us (0.75); the launches traced: 410 us -> 310 us
  blocking collectives: 50 us -> 0 us
  local copies, waits for them, and re-layouts: 61.6 us -> 30.7 us
  Pallas kernels: 237 us -> 215 us
    psum x1 -> x0, blocking collectives: 50 us -> none  [on_device(): vec_total = lax.psum(vec_sums, ('ctx', 'fsdp'))]
    pallas_call x6 -> x5, Pallas kernels: 227 us -> 205 us  [comm(): pl.pallas_call(kernel, name='comm%d' % cid, out_shape=[jax.ShapeDtypeStru...]
    convert_element_type x4 -> x0, local copies, waits for them, and re-layouts: 19.7 us -> none  [the longest x3 16.9 us: on_device(): d_qkv = got['qkv_o'].reshape(C, F, R, 3, DF).transpose(0, 2, 3, 1, 4).res...]
    dynamic_slice x9 -> x0, local copies, waits for them, and re-layouts: 6.62 us -> none  [the longest x7 3.88 us: own_part(): lax.dynamic_slice_in_dim(vec_total[start:start + size], f_index * (size /...]
    unnamed x91 -> x92, local copies, waits for them, and re-layouts: 9.03 us -> 5.67 us
where the time goes in v2:
time: 311 us; the launch traced here: 310 us
  Pallas kernels  215 us (69%)
  other arithmetic  38.3 us (12%)
  local copies, waits for them, and re-layouts  30.7 us (10%)
  matrix products  24.8 us (8%)
    pallas_call x5, Pallas kernels, comm(): pl.pallas_call(kernel, name='comm%d' % cid, out_shape=[jax.ShapeDtypeStru...  205 us
    dot_general x4, matrix products, dot_tn(): lax.dot_general(a, b, (((0,), (0,)), ((), ())), preferred_element_type=F32)  10.1 us
    another operation x12, local copies, waits for them, and re-layouts, rotary_tables(): return tuple((jnp.tile(t, (1, width // HD)) for t in (cos_t, sa, sb)))  9.95 us
    pallas_call x1, Pallas kernels, attention(): pl.pallas_call(attention_kernel, name='attention', out_shape=jax.ShapeDty...  9.82 us
    dot_general x4, matrix products, dot(): return jnp.dot(a, b, preferred_element_type=F32)  8.34 us
    dot_general x4, matrix products, dot_nt(): lax.dot_general(a, b, (((1,), (1,)), ((), ())), preferred_element_type=F32)  6.4 us

profile of v2, /device:TPU:0, one launch (start us, length us, event | category | flops | bytes accessed | tf_op | source)
XLA Modules:
  0.0 309.8 jit_solution(4468473658795017426)
XLA Ops:
  0.7 1.3 reduce_sum.174
  2.1 1.2 multiply_reduce_fusion
  3.3 1.9 fusion.31.args_3_
  5.2 0.7 fusion.41
  7.4 0.6 bitcast_convert_fusion.4.args_2_
  8.0 68.6 %comm1.1 = (bf16[4,128,1024]{2,1,0:T(8,128)(2,1)}, bf16[4,128,1024]{2,1,0:T(8,128)(2,1)}, f32[4,24,128]{2,1,0:T(8,128)}, bf16[4,4,2,32,1792]{4,3,2,1,0:T(8,128)(2,1)}) custom-call(bf16[8,32,3072]{2,1,0:T(8,128)(2,1)} %bitcast.147, bf16[8,32,4096]{2,1,0:T(8,128)(2,1)} %bitcast.143, f32[24,128]{1,0:T(8,128)} %bitcast_convert_fusion.4.args_2_, ...), custom_call_target="tpu_custom_call" | custom-call | tf_op jit(solution)/shard_map/comm1/pallas_call | solution.py:199
  76.6 0.8 copy.64
  77.5 2.7 fusion.8
  80.3 0.9 copy-done.9
  81.2 2.4 convolution_add_fusion
  83.6 1.5 fusion.40
  85.1 0.9 fusion.39
  86.3 0.7 tile.36
  87.0 1.1 copy.33
  88.1 0.7 tile.79
  88.8 1.8 copy.34
  90.6 0.7 tile.83
  91.3 1.8 copy.35
  93.1 2.5 fusion.23
  95.7 1.1 slice.213
  96.8 0.5 convolution_convert_fusion.4
  97.4 1.5 reshape.285
  99.0 2.5 copy.37
  101.5 3.0 multiply_convert_fusion
  104.5 2.2 fusion.42
  106.8 2.6 convolution_convert_fusion.1
  109.4 2.6 convolution_convert_fusion
  112.0 18.7 %comm2.1 = (bf16[4,8,128,128]{3,2,1,0:T(8,128)(2,1)}, bf16[4,4,32,1024]{3,2,1,0:T(8,128)(2,1)}, bf16[4,128,1024]{2,1,0:T(8,128)(2,1)}) custom-call(bf16[8,4,128,128]{3,2,1,0:T(8,128)(2,1)} %bitcast.137, bf16[4,4,2,32,1024]{4,3,2,1,0:T(8,128)(2,1)} %bitcast.133, bf16[4,2,128,1024]{3,2,1,0:T(8,128)(2,1)} %bitcast.135), custom_call_target="tpu_custom_call" | custom-call | tf_op jit(solution)/shard_map/comm2/pallas_call | solution.py:199
  130.7 3.1 %fusion.11.args_5_ = bf16[4,128,1024]{2,1,0:T(8,128)(2,1)} fusion(bf16[4,128,1024]{2,1,0:T(8,128)(2,1)} %get-tuple-element.38, bf16[4,2,128,1024]{3,2,1,0:T(8,128)(2,1)} %bitcast.136, s32[]{:T(128)S(6)} %select_n.23), kind=kLoop, calls=%fused_computation.21 | loop fusion | flops 2097152 | bytes 3145732 | tf_op jit(solution)/shard_map/convert_element_type | solution.py:438
  133.8 1.4 fusion.20.args_4_
  135.6 1.0 copy.38.cos_ref
  136.7 1.0 copy.39.sa_ref
  137.7 1.0 copy.40.sb_ref
  138.7 9.8 %attention.1 = bf16[4,1024,128]{2,1,0:T(8,128)(2,1)} custom-call(bf16[4,1024,128]{2,1,0:T(8,128)(2,1)} %bitcast.149, f32[1024,128]{1,0:T(8,128)} %copy.38.cos_ref, f32[1024,128]{1,0:T(8,128)} %copy.39.sa_ref, f32[1024,128]{1,0:T(8,128)} %copy.40.sb_ref), custom_call_target="tpu_custom_call" | custom-call | tf_op jit(solution)/shard_map/attention/pallas_call | solution.py:277
  148.5 16.9 %comm3.1 = bf16[4,8,128,128]{3,2,1,0:T(8,128)(2,1)} custom-call(bf16[4,8,128,128]{3,2,1,0:T(8,128)(2,1)} %bitcast.138), custom_call_target="tpu_custom_call" | custom-call | tf_op jit(solution)/shard_map/comm3/pallas_call | solution.py:199
  165.4 3.3 %copy.62 = bf16[4,4,2,128,128]{4,2,0,3,1:T(2,128)(2,1)} copy(bf16[4,4,2,128,128]{4,3,2,1,0:T(8,128)(2,1)} %bitcast.139) | data formatting | bytes 2097152 | tf_op jit(solution)/shard_map/reshape | solution.py:491
  168.7 2.0 reshape.292
  170.7 3.5 %convolution_convert_fusion.2 = bf16[1024,768]{1,0:T(8,128)(2,1)} fusion(bf16[512,1024]{1,0:T(8,128)(2,1)} %copy-done.9, bf16[512,1024]{1,0:T(8,128)(2,1)S(1)} %reshape.292), kind=kOutput, calls=%fused_computation.34 | convolution fusion | flops 806092800 | bytes 3407872 | tf_op jit(solution)/shard_map/dot_general | solution.py:311
  174.3 1.0 fusion.17
  175.5 0.3 copy-done.35
  175.8 2.7 fusion.37
  179.0 0.6 copy.63
  179.6 2.5 fusion.43
  182.2 0.5 add_convert_fusion.1
  182.6 0.8 copy-done.15
  183.4 1.5 pad_maximum_fusion.args_0_
  184.9 1.3 convolution_convert_fusion.3
  186.2 45.0 %comm4.1 = (bf16[4,2,128,1024]{3,2,1,0:T(8,128)(2,1)}, f32[4,24,128]{2,1,0:T(8,128)}, bf16[4,4,32,1024]{3,2,1,0:T(8,128)(2,1)}, bf16[4,128,1024]{2,1,0:T(8,128)(...) custom-call(bf16[4,2,128,1024]{3,2,1,0:T(8,128)(2,1)} %pad_maximum_fusion.args_0_, ...), custom_call_target="tpu_custom_call" | custom-call | tf_op jit(solution)/shard_map/comm4/pallas_call | solution.py:199
  231.2 2.3 reduce_sum.186.args_0_
  233.4 2.2 reduce_sum.188.args_2_
  235.6 0.8 reduce_sum.187.args_1_
  236.5 0.7 reduce_sum.189.args_3_
  237.1 0.6 reduce_sum.190.args_4_
  237.7 55.8 %comm6.1 = (bf16[4,2,32,4096]{3,2,1,0:T(8,128)(2,1)}, bf16[4,2,32,3072]{3,2,1,0:T(8,128)(2,1)}, bf16[4,2,128,1024]{3,2,1,0:T(8,128)(2,1)}, bf16[4,2,32,1024]{3,2,1,0:T(8,128)(2,1)}, f32[8,24,128]{2,1,0:T(8,128)}) custom-call(bf16[4,32,1024]{2,1,0:T(8,128)(2,1)} %reduce_sum.186.args_0_, bf16[4,32,768]{2,1,0:T(8,128)(2,1)} %reduce_sum.187.args_1_, ...), custom_call_target="tpu_custom_call" | custom-call | tf_op jit(solution)/shard_map/comm6/pallas_call | solution.py:199
  293.6 4.2 %bitcast_convert_fusion = f32[1024,1024]{1,0:T(8,128)} fusion(bf16[4,2,128,1024]{3,2,1,0:T(8,128)(2,1)} %get-tuple-element.49), kind=kLoop, calls=%fused_computation.18 | loop fusion | flops 1048576 | bytes 6291456 | tf_op jit(solution)/shard_map/convert_element_type | solution.py:647
  297.8 2.6 bitcast_convert_fusion.1
  300.5 2.1 bitcast_convert_fusion.2
  302.6 1.1 bitcast_convert_fusion.3
  303.7 0.6 slice_bitcast_fusion.6
  304.3 0.6 slice_bitcast_fusion
  304.9 0.6 slice_bitcast_fusion.1
  305.5 2.2 convert_reduce_fusion
  308.1 1.1 multiply_add_fusion
  309.2 0.6 copy.79
  (129 shorter events, 3.7 us)
Async XLA Ops:
  0.6 103.9 %copy-start = (bf16[1024,1024]{1,0:T(8,128)(2,1)S(1)}, bf16[1024,1024]{1,0:T(8,128)(2,1)}, u32[]{:S(2)}) copy-start(bf16[1024,1024]{1,0:T(8,128)(2,1)} %param.25) | copy-start | bytes 6291460
  0.7 4.5 %copy-start.5 = (f32[1,128,1024]{2,1,0:T(8,128)S(1)}, f32[1,128,1024]{2,1,0:T(8,128)}, u32[]{:S(2)}) copy-start(f32[1,128,1024]{2,1,0:T(8,128)} %param.27) | copy-start | bytes 1572868
  0.7 5.3 %copy-start.26 = (bf16[256]{0:T(256)(128)(2,1)S(1)}, bf16[256]{0:T(256)(128)(2,1)}, u32[]{:S(2)}) copy-start(bf16[256]{0:T(256)(128)(2,1)} %param.15) | copy-start | bytes 1540
  0.7 5.4 %copy-start.27 = (bf16[256]{0:T(256)(128)(2,1)S(1)}, bf16[256]{0:T(256)(128)(2,1)}, u32[]{:S(2)}) copy-start(bf16[256]{0:T(256)(128)(2,1)} %param.16) | copy-start | bytes 1540
  0.7 5.6 %copy-start.28 = (bf16[256]{0:T(256)(128)(2,1)S(1)}, bf16[256]{0:T(256)(128)(2,1)}, u32[]{:S(2)}) copy-start(bf16[256]{0:T(256)(128)(2,1)} %param.17) | copy-start | bytes 1540
  0.7 5.9 %copy-start.29 = (bf16[256]{0:T(256)(128)(2,1)S(1)}, bf16[256]{0:T(256)(128)(2,1)}, u32[]{:S(2)}) copy-start(bf16[256]{0:T(256)(128)(2,1)} %param.18) | copy-start | bytes 1540
  0.7 6.1 %copy-start.30 = (bf16[256]{0:T(256)(128)(2,1)S(1)}, bf16[256]{0:T(256)(128)(2,1)}, u32[]{:S(2)}) copy-start(bf16[256]{0:T(256)(128)(2,1)} %param.22) | copy-start | bytes 1540
  0.7 6.3 %copy-start.31 = (bf16[256]{0:T(256)(128)(2,1)S(1)}, bf16[256]{0:T(256)(128)(2,1)}, u32[]{:S(2)}) copy-start(bf16[256]{0:T(256)(128)(2,1)} %param.26) | copy-start | bytes 1540
  0.7 6.5 %copy-start.25 = (bf16[768]{0:T(1024)(128)(2,1)S(1)}, bf16[768]{0:T(1024)(128)(2,1)}, u32[]{:S(2)}) copy-start(bf16[768]{0:T(1024)(128)(2,1)} %param.20) | copy-start | bytes 4612
  80.2 1.0 copy-start.9
  83.6 1.5 copy-start.2
  93.1 3.6 %copy-start.11 = (bf16[4,128,1024]{2,1,0:T(8,128)(2,1)S(1)}, bf16[4,128,1024]{2,1,0:T(8,128)(2,1)}, u32[]{:S(2)}) copy-start(bf16[4,128,1024]{2,1,0:T(8,128)(2,1)} %get-tuple-element.35) | copy-start | bytes 3145732
  93.1 3.6 %copy-start.17 = (bf16[256,1024]{1,0:T(8,128)(2,1)S(1)}, bf16[256,1024]{1,0:T(8,128)(2,1)}, u32[]{:S(2)}) copy-start(bf16[256,1024]{1,0:T(8,128)(2,1)} %param.21) | copy-start | bytes 1572868
  97.4 4.1 %copy-start.24 = (bf16[1024]{0:T(1024)(128)(2,1)S(1)}, bf16[1024]{0:T(1024)(128)(2,1)}, u32[]{:S(2)}) copy-start(bf16[1024]{0:T(1024)(128)(2,1)} %param.24) | copy-start | bytes 6148
  99.0 2.5 copy-start.10
  101.5 3.0 copy-start.12
  104.5 4.9 %copy-start.33 = (bf16[512,1024]{1,0:T(8,128)(2,1)}, bf16[512,1024]{1,0:T(8,128)(2,1)S(1)}, u32[]{:S(2)}) copy-start(bf16[512,1024]{1,0:T(8,128)(2,1)S(1)} %get-tuple-element.87) | copy-start | bytes 3145732
  106.7 2.6 copy-start.34
  130.7 3.1 %copy-start.14 = (bf16[4,4,32,1024]{3,2,1,0:T(8,128)(2,1)S(1)}, bf16[4,4,32,1024]{3,2,1,0:T(8,128)(2,1)}, u32[]{:S(2)}) copy-start(bf16[4,4,32,1024]{3,2,1,0:T(8,128)(2,1)} %get-tuple-element.37) | copy-start | bytes 3145732
  130.7 3.1 %copy-start.3 = (bf16[1024,1024]{1,0:T(8,128)(2,1)S(1)}, bf16[1024,1024]{1,0:T(8,128)(2,1)}, u32[]{:S(2)}) copy-start(bf16[1024,1024]{1,0:T(8,128)(2,1)} %convolution_convert_fusion.1) | copy-start | bytes 6291460
  170.7 3.5 %copy-start.32 = (bf16[4,4,2,32,1792]{4,3,2,1,0:T(8,128)(2,1)S(1)}, bf16[4,4,2,32,1792]{4,3,2,1,0:T(8,128)(2,1)}, u32[]{:S(2)}) copy-start(bf16[4,4,2,32,1792]{4,3,2,1,0:T(8,128)(2,1)} %get-tuple-element.34) | copy-start | bytes 11010052
  174.3 1.2 copy-start.8
  174.3 1.5 copy-start.35
  179.6 2.5 copy-start.18
  182.2 1.2 copy-start.15
  183.4 1.5 copy-start.13
  231.1 4.5 %copy-start.16 = (bf16[4,4,32,768]{3,2,1,0:T(8,128)(2,1)S(1)}, bf16[4,4,32,768]{3,2,1,0:T(8,128)(2,1)}, u32[]{:S(2)}) copy-start(bf16[4,4,32,768]{3,2,1,0:T(8,128)(2,1)} %get-tuple-element.41) | copy-start | bytes 2359300
  231.2 5.3 %copy-start.20 = (bf16[4,32,1024]{2,1,0:T(8,128)(2,1)S(1)}, bf16[4,32,1024]{2,1,0:T(8,128)(2,1)}, u32[]{:S(2)}) copy-start(bf16[4,32,1024]{2,1,0:T(8,128)(2,1)} %get-tuple-element.43) | copy-start | bytes 786436
  231.2 6.0 %copy-start.22 = (f32[4,24,128]{2,1,0:T(8,128)S(1)}, f32[4,24,128]{2,1,0:T(8,128)}, u32[]{:S(2)}) copy-start(f32[4,24,128]{2,1,0:T(8,128)} %get-tuple-element.44) | copy-start | bytes 147460
  293.6 4.2 %copy-start.4 = (bf16[4,2,32,4096]{3,2,1,0:T(8,128)(2,1)S(1)}, bf16[4,2,32,4096]{3,2,1,0:T(8,128)(2,1)}, u32[]{:S(2)}) copy-start(bf16[4,2,32,4096]{3,2,1,0:T(8,128)(2,1)} %get-tuple-element.48) | copy-start | bytes 6291460
  297.8 2.6 copy-start.7
  300.5 2.1 copy-start.19
  300.5 3.3 %copy-start.21 = (f32[8,24,128]{2,1,0:T(8,128)S(1)}, f32[8,24,128]{2,1,0:T(8,128)}, u32[]{:S(2)}) copy-start(f32[8,24,128]{2,1,0:T(8,128)} %get-tuple-element.45) | copy-start | bytes 294916
  302.6 5.1 %copy-start.1 = (f32[1,128,1024]{2,1,0:T(8,128)S(1)}, f32[1,128,1024]{2,1,0:T(8,128)}, u32[]{:S(2)}) copy-start(f32[1,128,1024]{2,1,0:T(8,128)} %param.14) | copy-start | bytes 1572868
  304.3 4.9 %copy-start.23 = (f32[256]{0:T(256)}, f32[256]{0:T(256)S(1)}, u32[]{:S(2)}) copy-start(f32[256]{0:T(256)S(1)} %get-tuple-element.122) | copy-start | bytes 3076
  305.5 2.6 copy-start.6
